TPU v7x, 32 devices: a whole 2x2x4 slice. The times are simulated.
32 devices in a mesh: comp: 4 (over y, x), samp: 8 (over z, core).
Axes of the slice: x: 2, y: 2, z: 4, core: 2. Of those that a mesh axis runs over, the one named last changes fastest.
Arguments:
- samples: float32 [2048, 32768], P('comp', 'samp'), may hold values from -1.7 to 1.7
- unmixing: float32 [2048, 2048], P('comp', 'samp'), may hold values from -0.37565048 to 0.37565048, as said below
Outputs:
- decorrelated: float32 [2048, 2048], P('comp', 'samp')
Inputs may be any that keep to these rules, and one draw needn't show every extreme that they name: `unmixing`: every entry's magnitude is at most 17 / sqrt(2048).
All inputs are finite; a program needn't handle non-finite values.
Results may differ from a plain program's by a relative error of at most 0.00011.
Values sent between devices are 32-bit elements; how exact they have to be, the bound alone decides.
No kernel may reach another device: no remote copies, remote signals or barrier semaphores. Data moves between devices by JAX's collectives and lax.ppermute only.
A program may use at most 128 MiB of HBM per device.

v0:
```python
import functools

import jax
import jax.numpy as jnp
from jax import lax
from jax.experimental import pallas as pl
from jax.experimental.pallas import tpu as pltpu
from jax.sharding import PartitionSpec as P


NS_STEPS = 3
AXES = ("comp", "samp")
CHUNKS = 4
BLOCKS = 2
LANES = 128
VMEM_BYTES = 60 * 2**20
f32, bf16 = jnp.float32, jnp.bfloat16


def split(v):
    hi = v.astype(bf16)
    return hi, (v - hi.astype(f32)).astype(bf16)


def dot(a, b):
    return jnp.dot(a, b, preferred_element_type=f32)


def dot_nt(a, b):
    return lax.dot_general(a, b, (((1,), (1,)), ((), ())), preferred_element_type=f32)


def weights_kernel(n_z, *refs):
    pieces, (wh, wl) = refs[:-2], refs[-2:]
    z = lax.axis_index("samp") // 2
    rows, width = pieces[0].shape
    for r in range(2):
        for dz in range(n_z):
            hi, lo = split(pieces[r * n_z + dz][...])
            col = pl.multiple_of((z ^ dz) * width, width)
            wh[r * rows : (r + 1) * rows, pl.ds(col, width)] = hi
            wl[r * rows : (r + 1) * rows, pl.ds(col, width)] = lo


def assemble_weights(pieces, n_z):
    rows, width = pieces[0].shape
    shape = jax.ShapeDtypeStruct((2 * rows, n_z * width), bf16)
    return pl.pallas_call(
        functools.partial(weights_kernel, n_z),
        out_shape=(shape, shape),
        in_specs=[pl.BlockSpec(memory_space=pltpu.VMEM)] * len(pieces),
        out_specs=(pl.BlockSpec(memory_space=pltpu.VMEM),) * 2,
        compiler_params=pltpu.CompilerParams(vmem_limit_bytes=VMEM_BYTES),
        cost_estimate=pl.CostEstimate(
            flops=4 * rows * width * len(pieces),
            transcendentals=0,
            bytes_accessed=8 * rows * width * len(pieces),
        ),
    )(*pieces)


def moment_kernel(first, n_p, *refs):
    pieces, refs = refs[:n_p], refs[n_p:]
    if first:
        wh, wl, m_out, s_out, xh, xl = refs
    else:
        wh, wl, m_in, s_in, m_out, s_out, xh, xl = refs
    rows, size = pieces[0].shape
    c = lax.axis_index("comp")

    @pl.when(pl.program_id(0) == 0)
    def _():
        for i, piece in enumerate(pieces):
            hi, lo = split(piece[...])
            place = pl.ds(pl.multiple_of((c ^ (i // 2)) * rows, rows), rows)
            cols = slice(i % 2 * size, (i % 2 + 1) * size)
            xh[place, cols] = hi
            xl[place, cols] = lo

    t = jnp.tanh(dot(wh[...], xh[...]) + dot(wh[...], xl[...]) + dot(wl[...], xh[...]))
    d = 1.0 - t * t
    part = d[:, :LANES]
    for q in range(1, d.shape[1] // LANES):
        part = part + d[:, q * LANES : (q + 1) * LANES]
    s_out[...] = part if first else s_in[...] + part
    th, tl = split(t)
    m = dot_nt(th, xh[...]) + dot_nt(th, xl[...]) + dot_nt(tl, xh[...])
    m_out[...] = m if first else m_in[...] + m


def moment_chunk(pieces, wh, wl, state):
    n_rows, order = wh.shape
    rows, size = pieces[0].shape
    block = n_rows // BLOCKS
    first = state is None
    carried = [] if first else list(state)
    n_p = len(pieces)

    def by_rows(n):
        return pl.BlockSpec((block, n), lambda i: (i, 0))

    once = pl.BlockSpec((rows, size), lambda i: (0, 0), pipeline_mode=pl.Buffered(1))
    return pl.pallas_call(
        functools.partial(moment_kernel, first, n_p),
        grid=(BLOCKS,),
        out_shape=(
            jax.ShapeDtypeStruct((n_rows, order), f32),
            jax.ShapeDtypeStruct((n_rows, LANES), f32),
        ),
        in_specs=[once] * n_p
        + [by_rows(order)] * 2
        + ([] if first else [by_rows(order), by_rows(LANES)]),
        out_specs=(by_rows(order), by_rows(LANES)),
        scratch_shapes=[pltpu.VMEM((order, 2 * size), bf16)] * 2,
        input_output_aliases={} if first else {n_p + 2: 0, n_p + 3: 1},
        compiler_params=pltpu.CompilerParams(
            vmem_limit_bytes=VMEM_BYTES, dimension_semantics=("arbitrary",)
        ),
        cost_estimate=pl.CostEstimate(
            flops=24 * n_rows * order * size,
            transcendentals=2 * n_rows * size,
            bytes_accessed=8 * order * size + 12 * n_rows * order,
        ),
    )(*pieces, wh, wl, *carried)


def schedule(steps):
    products = []

    def advance(level, src, held):
        held = held | {src}
        inner = src
        for k in reversed(range(level)):
            for _ in range(2):
                inner = advance(k, inner, held)
        into = min(set(range(8)) - held - {inner})
        products.append((into, inner, src))
        return into

    value = 0
    for level in range(steps):
        value = advance(level, value, frozenset())
    return products, value


def newton_kernel(last, block, rows, places, n_in, *refs):
    table, pieces, out_ref = refs[0], refs[1 : n_in + 1], refs[n_in + 1]
    stage, uh, ul, gh, gl, rhs, vectors, squares, sem = refs[n_in + 2 :]
    order = uh.shape[0]
    tall, lanes = rhs.shape[0], rhs.shape[0] // 2
    size = pieces[0].shape[0]
    n = order // block
    c, s = lax.axis_index("comp"), lax.axis_index("samp")
    z, core = s // 2, s % 2
    first = (s * (lax.axis_size("comp") * lanes)) + c * lanes
    aligned = pl.multiple_of(first // LANES * LANES, LANES)
    shift = lax.rem(LANES - (first - aligned), LANES)
    slots = stage.shape[0]

    def copy(i):
        return pltpu.make_async_copy(pieces[i], stage.at[i % slots], sem.at[i % slots])

    for i in range(slots - 1):
        copy(i).start()
    squares[...] = jnp.zeros_like(squares)
    for i in range(n_in):
        if i + slots - 1 < n_in:
            copy(i + slots - 1).start()
        copy(i).wait()
        r, dz, dk = places[i]
        start = (core ^ dk) * (rows // 2)
        span, bit = rows // 2, 1
        while span > size:
            span //= 2
            start = start + (((z ^ dz) // bit) % 2) * span
            bit *= 2
        start = r * rows + start

        @pl.loop(0, size // 16)
        def _(q):
            here = pl.ds(pl.multiple_of(start + q * 16, 16), 16)
            v = stage[i % slots, pl.ds(pl.multiple_of(q * 16, 16), 16), :]
            part = v * v
            total = part[:, :LANES]
            for t in range(1, order // LANES):
                total = total + part[:, t * LANES : (t + 1) * LANES]
            squares[...] += total
            hi, lo = split(v)
            uh[here, :] = hi
            ul[here, :] = lo

    @pl.loop(0, order // block)
    def _(b):
        here = pl.ds(pl.multiple_of(b * block, block), block)
        cols = pl.ds(aligned, LANES)
        v = uh[here, cols].astype(f32) + ul[here, cols].astype(f32)
        v = pltpu.roll(v, shift, 1).T[:lanes]
        vectors[0, :lanes, here] = v
        vectors[0, lanes:, here] = v

    @pl.loop(0, n)
    def _(i):
        here = pl.ds(pl.multiple_of(i * block, block), block)

        @pl.loop(0, i + 1)
        def _(j):
            there = pl.ds(pl.multiple_of(j * block, block), block)
            g = dot_nt(uh[here, :], uh[there, :])
            g += dot_nt(uh[here, :], ul[there, :])
            g += dot_nt(ul[here, :], uh[there, :])
            hi, lo = split(g)
            gh[here, there] = hi
            gl[here, there] = lo

            @pl.when(j < i)
            def _():
                hi, lo = split(g.T)
                gh[there, here] = hi
                gl[there, here] = lo

    scale2 = 6.25 * (jnp.sum(squares[...]) / order + 1e-06)
    upper = lax.broadcasted_iota(jnp.int32, (tall, order), 0) < lanes
    tile = order // 2

    @pl.loop(0, table.shape[0] // 3)
    def _(p):
        into, src, base = table[3 * p], table[3 * p + 1], table[3 * p + 2]
        hi, lo = split(vectors[src])
        rhs[...] = jnp.where(upper, hi, lo)

        @pl.loop(0, order // tile)
        def _(b):
            cols = pl.ds(pl.multiple_of(b * tile, tile), tile)
            e = dot(rhs[...], gh[:, cols]) + dot(rhs[...], gl[:, cols])
            e = e + jnp.concatenate([e[lanes:], e[:lanes]], axis=0)
            vectors[into, :, cols] = 1.5 * vectors[base, :, cols] - (0.5 / scale2) * e

    out_ref[...] = vectors[last, :lanes] * (jnp.sqrt(jnp.float32(order)) / jnp.sqrt(scale2))


def newton(pieces, places, rows, share):
    size, order = pieces[0].shape
    block = min(256, order)
    square = pltpu.VMEM((order, order), bf16)
    products, last = schedule(NS_STEPS)
    n_buffers = 1 + max(into for into, _, _ in products)
    table = jnp.array([i for p in products for i in p], jnp.int32)
    return pl.pallas_call(
        functools.partial(newton_kernel, last, block, rows, places, len(pieces)),
        out_shape=jax.ShapeDtypeStruct((share, order), f32),
        in_specs=[pl.BlockSpec(memory_space=pltpu.SMEM)]
        + [pl.BlockSpec(memory_space=pl.ANY)] * len(pieces),
        out_specs=pl.BlockSpec(memory_space=pltpu.VMEM),
        scratch_shapes=[pltpu.VMEM((4, size, order), f32)]
        + [square] * 4
        + [
            pltpu.VMEM((2 * share, order), bf16),
            pltpu.VMEM((n_buffers, 2 * share, order), f32),
            pltpu.VMEM((16, LANES), f32),
            pltpu.SemaphoreType.DMA((4,)),
        ],
        compiler_params=pltpu.CompilerParams(vmem_limit_bytes=VMEM_BYTES),
    )(table, *pieces)


def spread(n_z, n_c):
    every = [(dz, r) for dz in range(n_z) for r in range(n_c)]
    return sorted(every, key=lambda p: (p[0].bit_count() + p[1].bit_count(), p[1], p[0]))


def on_device(samples, unmixing):
    n_c, n_s = lax.axis_size("comp"), lax.axis_size("samp")
    c, s = lax.axis_index("comp"), lax.axis_index("samp")
    x, core, z = c % 2, s % 2, s // 2
    n_z = n_s // 2
    z_bits = [1 << i for i in range(n_z.bit_length() - 1)]
    rows, n_local = samples.shape
    width = unmixing.shape[1]
    order = width * n_s
    count = n_local * n_s
    share = width // n_c

    def swap(value, comp_bits=0, samp_bits=0):
        pairs = [
            (i * n_s + j, (i ^ comp_bits) * n_s + (j ^ samp_bits))
            for i in range(n_c)
            for j in range(n_s)
        ]
        return lax.ppermute(value, AXES, pairs)

    def gather_z(piece, bits):
        found = {0: piece}
        for bit in bits:
            found |= {dz ^ bit: swap(p, samp_bits=2 * bit) for dz, p in found.items()}
        return [found[dz] for dz in range(n_z)]

    lower = rows // 2
    own_half = lax.dynamic_slice_in_dim(unmixing, core * lower, lower, 0)
    other_half = lax.dynamic_slice_in_dim(unmixing, (1 - core) * lower, lower, 0)
    other_half = swap(other_half, samp_bits=1)
    own_half = jnp.where(
        core == 0,
        jnp.concatenate([own_half, other_half], axis=1),
        jnp.concatenate([other_half, own_half], axis=1),
    )
    near_half = swap(own_half, comp_bits=1)

    half = n_local // 2
    size = half // CHUNKS
    chunks = [[None] * n_c for _ in range(CHUNKS)]
    for j, pieces in enumerate(chunks):
        sent = lax.dynamic_slice_in_dim(samples, (1 - x) * half + j * size, size, 1)
        pieces[1] = swap(sent, comp_bits=1)
        pieces[0] = lax.dynamic_slice_in_dim(samples, x * half + j * size, size, 1)
        for r in range(2, n_c, 2):
            pieces[r] = swap(pieces[0], comp_bits=r)
        for r in range(2, n_c, 2):
            pieces[r + 1] = swap(pieces[1], comp_bits=r)

    w_own = gather_z(own_half, z_bits)
    w_pieces = w_own + gather_z(near_half, z_bits[::-1])
    wh, wl = assemble_weights(w_pieces, n_z)

    state = None
    for pieces in chunks:
        both = []
        for r in range(n_c):
            both += [pieces[r], swap(pieces[r], samp_bits=1)]
        state = moment_chunk(both, wh, wl, state)
    moment, slope = state

    slope = jnp.sum(slope, axis=1).reshape(2, lower)
    slope = slope + swap(slope, comp_bits=1)[::-1]
    for bit in z_bits:
        slope = slope + swap(slope, samp_bits=2 * bit)

    def halve_comp(value):
        return value[0] + swap(value[1], comp_bits=1)

    def halve_z(value, bit):
        side, axis = (z // bit) % 2, value.ndim - 2
        size = value.shape[axis] // 2
        mine = lax.dynamic_slice_in_dim(value, side * size, size, axis)
        sent = lax.dynamic_slice_in_dim(value, (1 - side) * size, size, axis)
        return mine + swap(sent, samp_bits=2 * bit)

    moment = moment.reshape(2, lower, order)
    front, back = moment[:, :, : order // 2], moment[:, :, order // 2 :]
    front, back = halve_comp(front), halve_z(back, z_bits[0])
    front, back = halve_z(front, z_bits[0]), halve_comp(back)
    for bit in z_bits[1:]:
        front, back = halve_z(front, bit), halve_z(back, bit)
    moment = jnp.concatenate([front, back], axis=1)

    size = moment.shape[0]
    start, span = 0, lower
    for bit in z_bits:
        span //= 2
        start = start + ((z // bit) % 2) * span
    own_slope = lax.dynamic_slice_in_dim(slope[0], start, size, 0) / count
    own_rows = [lax.dynamic_slice_in_dim(p, start, size, 0) for p in w_own]
    for bit in z_bits:
        own_rows = [
            jnp.where((z // bit) % 2 == 0, own_rows[i], own_rows[i ^ bit]) for i in range(n_z)
        ]
    updated = moment / count - own_slope[:, None] * jnp.concatenate(own_rows, axis=1)

    c_bits = [1 << i for i in range(n_c.bit_length() - 1)]
    rows_of = {(0, 0): updated}
    for bit in z_bits[::-1]:
        for dz, _ in list(rows_of):
            rows_of[dz ^ bit, 0] = swap(rows_of[dz, 0], samp_bits=2 * bit)
    for dz in range(n_z):
        for bit in c_bits if dz % 2 else c_bits[::-1]:
            for r in [r for d, r in list(rows_of) if d == dz]:
                rows_of[dz, r ^ bit] = swap(rows_of[dz, r], comp_bits=bit)
    pieces, places = [], []
    for dz, r in spread(n_z, n_c):
        pieces += [rows_of[dz, r], swap(rows_of[dz, r], samp_bits=1)]
        places += [(r, dz, 0), (r, dz, 1)]

    current = newton(pieces, tuple(places), rows, share)

    got = [current[:, :rows]]
    got += [swap(current[:, r * rows : (r + 1) * rows], comp_bits=r) for r in range(1, n_c)]
    bit = 1
    while bit < n_c:
        got = [jnp.where((c // bit) % 2 == 0, got[i], got[i ^ bit]) for i in range(n_c)]
        bit *= 2
    return jnp.concatenate(got, axis=0).T


def solution(mesh):
    return jax.shard_map(
        on_device,
        mesh=mesh,
        in_specs=(P("comp", "samp"), P("comp", "samp")),
        out_specs=P("comp", "samp"),
        check_vma=False,
    )
```

profile of v0, /device:TPU:0, one launch (start us, length us, event | category | flops | bytes accessed | tf_op | source)
XLA Modules:
  0.0 554.4 jit_solution(11070830984531051139)
XLA Ops:
  5.8 5.5 constant_dynamic-slice_fusion.6
  18.5 19.1 %collective-permute-done.8.refs_1_ = f32[256,512]{1,0:T(8,128)S(1)} collective-permute-done((f32[256,512]{1,0:T(8,128)S(1)}, f32[256,512]{1,0:T(8,128)S(1)}, u32[]{:S(2)}, u32[]{:S(2)}) %collective-permute-start.8) | collective-permute-done | bytes 524320 | tf_op jit(solution)/shard_map/ppermute | solution.py:289
  45.6 18.1 %collective-permute-done.23.refs_2_ = f32[512,512]{1,0:T(8,128)} collective-permute-done((f32[512,512]{1,0:T(8,128)S(1)}, f32[512,512]{1,0:T(8,128)}, u32[]{:S(2)}, u32[]{:S(2)}) %collective-permute-start.23) | collective-permute-done | bytes 1048608 | tf_op jit(solution)/shard_map/ppermute | solution.py:289
  63.8 2.9 collective-permute-start.13
  68.6 16.8 %collective-permute-done.16.refs_2_ = f32[512,512]{1,0:T(8,128)S(1)} collective-permute-done((f32[512,512]{1,0:T(8,128)S(1)}, f32[512,512]{1,0:T(8,128)S(1)}, u32[]{:S(2)}, u32[]{:S(2)}) %collective-permute-start.16) | collective-permute-done | bytes 1048608 | tf_op jit(solution)/shard_map/ppermute | solution.py:289
  87.2 13.7 %collective-permute-done.13.refs_6_ = f32[256,512]{1,0:T(8,128)S(1)} collective-permute-done((f32[256,512]{1,0:T(8,128)S(1)}, f32[256,512]{1,0:T(8,128)S(1)}, u32[]{:S(2)}, u32[]{:S(2)}) %collective-permute-start.13) | collective-permute-done | bytes 524320 | tf_op jit(solution)/shard_map/ppermute | solution.py:289
  101.1 10.0 %collective-permute-done.10.refs_3_ = f32[256,512]{1,0:T(8,128)S(1)} collective-permute-done((f32[256,512]{1,0:T(8,128)S(1)}, f32[256,512]{1,0:T(8,128)S(1)}, u32[]{:S(2)}, u32[]{:S(2)}) %collective-permute-start.10) | collective-permute-done | bytes 524320 | tf_op jit(solution)/shard_map/ppermute | solution.py:289
  111.9 9.6 %collective-permute-done.12.refs_5_ = f32[256,512]{1,0:T(8,128)S(1)} collective-permute-done((f32[256,512]{1,0:T(8,128)S(1)}, f32[256,512]{1,0:T(8,128)S(1)}, u32[]{:S(2)}, u32[]{:S(2)}) %collective-permute-start.12) | collective-permute-done | bytes 524320 | tf_op jit(solution)/shard_map/ppermute | solution.py:289
  121.5 9.6 %collective-permute-done.14.refs_7_ = f32[256,512]{1,0:T(8,128)S(1)} collective-permute-done((f32[256,512]{1,0:T(8,128)S(1)}, f32[256,512]{1,0:T(8,128)S(1)}, u32[]{:S(2)}, u32[]{:S(2)}) %collective-permute-start.14) | collective-permute-done | bytes 524320 | tf_op jit(solution)/shard_map/ppermute | solution.py:289
  133.0 4.9 shard_map.37
  139.9 15.1 %collective-permute-done.27.refs_6_ = f32[512,512]{1,0:T(8,128)} collective-permute-done((f32[512,512]{1,0:T(8,128)}, f32[512,512]{1,0:T(8,128)}, u32[]{:S(2)}, u32[]{:S(2)}) %collective-permute-start.27) | collective-permute-done | bytes 1048608 | tf_op jit(solution)/shard_map/ppermute | solution.py:289
  156.7 19.9 %shard_map.38 = (f32[512,2048]{1,0:T(8,128)}, f32[512,128]{1,0:T(8,128)}) custom-call(f32[512,512]{1,0:T(8,128)} %copy-done.6, f32[512,512]{1,0:T(8,128)} %copy-done.49, f32[512,512]{1,0:T(8,128)} %collective-permute-done.30.refs_2_, f32[512,512]{1,0:T(8,128)} %collective-permute-done.31.refs_3_, f32[512,512]{1,0:T(8,128)} %collective-permute-done.32.refs_4_, ...), custom_call_target="tpu_custom_call" | custom-call | flops 12884901888 | bytes 20971520 | tf_op jit(solution)/shard_map/pallas_call | solution.py:103
  179.6 21.0 %shard_map.39 = (f32[512,2048]{1,0:T(8,128)}, f32[512,128]{1,0:T(8,128)}) custom-call(f32[512,512]{1,0:T(8,128)} %copy-done.5, f32[512,512]{1,0:T(8,128)} %copy-done.48, f32[512,512]{1,0:T(8,128)} %collective-permute-done.23.refs_2_, f32[512,512]{1,0:T(8,128)} %collective-permute-done.24.refs_3_, ...), custom_call_target="tpu_custom_call", output_to_operand_aliasing={{0}: (10, {}), {1}: (11, {})} | custom-call | flops 12884901888 | bytes 20971520 | tf_op jit(solution)/shard_map/pallas_call | solution.py:103
  203.3 21.4 %collective-permute-done.5.refs_6_ = f32[512,512]{1,0:T(8,128)S(1)} collective-permute-done((f32[512,512]{1,0:T(8,128)}, f32[512,512]{1,0:T(8,128)S(1)}, u32[]{:S(2)}, u32[]{:S(2)}) %collective-permute-start.5) | collective-permute-done | bytes 1048608 | tf_op jit(solution)/shard_map/ppermute | solution.py:289
  224.7 21.2 %shard_map.40 = (f32[512,2048]{1,0:T(8,128)}, f32[512,128]{1,0:T(8,128)}) custom-call(f32[512,512]{1,0:T(8,128)} %copy-done.4, f32[512,512]{1,0:T(8,128)} %collective-permute-done.15.refs_1_, f32[512,512]{1,0:T(8,128)} %copy-done.45, f32[512,512]{1,0:T(8,128)} %collective-permute-done.17.refs_3_, ...), custom_call_target="tpu_custom_call", output_to_operand_aliasing={{0}: (10, {}), {1}: (11, {})} | custom-call | flops 12884901888 | bytes 20971520 | tf_op jit(solution)/shard_map/pallas_call | solution.py:103
  245.9 21.3 %shard_map.41 = (f32[512,2048]{1,0:T(8,128)}, f32[512,128]{1,0:T(8,128)}) custom-call(f32[512,512]{1,0:T(8,128)} %copy-done.3, f32[512,512]{1,0:T(8,128)} %collective-permute-done.refs_1_, f32[512,512]{1,0:T(8,128)} %collective-permute-done.1.refs_2_, f32[512,512]{1,0:T(8,128)} %collective-permute-done.2.refs_3_, ...), custom_call_target="tpu_custom_call", output_to_operand_aliasing={{0}: (10, {}), {1}: (11, {})} | custom-call | flops 12884901888 | bytes 20971520 | tf_op jit(solution)/shard_map/pallas_call | solution.py:103
  273.0 21.0 %collective-permute-done.36 = f32[256,1024]{1,0:T(8,128)} collective-permute-done((f32[256,1024]{1,0:T(8,128)S(1)}, f32[256,1024]{1,0:T(8,128)}, u32[]{:S(2)}, u32[]{:S(2)}) %collective-permute-start.36) | collective-permute-done | bytes 1048608 | tf_op jit(solution)/shard_map/ppermute | solution.py:289
  302.9 10.6 %collective-permute-done.42 = f32[2,256]{1,0:T(2,128)S(1)} collective-permute-done((f32[2,256]{1,0:T(2,128)S(1)}, f32[2,256]{1,0:T(2,128)S(1)}, u32[]{:S(2)}, u32[]{:S(2)}) %collective-permute-start.42) | collective-permute-done | bytes 2080 | tf_op jit(solution)/shard_map/ppermute | solution.py:289
  314.3 3.0 collective-permute-done.43
  317.3 4.5 collective-permute-start.44
  324.5 3.0 collective-permute-start.38
  328.8 13.9 %collective-permute-done.38 = f32[64,1024]{1,0:T(8,128)S(1)} collective-permute-done((f32[64,1024]{1,0:T(8,128)S(1)}, f32[64,1024]{1,0:T(8,128)S(1)}, u32[]{:S(2)}, u32[]{:S(2)}) %collective-permute-start.38) | collective-permute-done | bytes 262176 | tf_op jit(solution)/shard_map/ppermute | solution.py:289
  342.7 4.4 collective-permute-done.41
  347.4 3.6 collective-permute-start.46
  352.2 20.1 %collective-permute-done.48.refs_5_ = f32[64,2048]{1,0:T(8,128)S(1)} collective-permute-done((f32[64,2048]{1,0:T(8,128)S(1)}, f32[64,2048]{1,0:T(8,128)S(1)}, u32[]{:S(2)}, u32[]{:S(2)}) %collective-permute-start.48) | collective-permute-done | bytes 524320 | tf_op jit(solution)/shard_map/ppermute | solution.py:289
  376.5 8.4 %collective-permute-done.54.refs_11_ = f32[64,2048]{1,0:T(8,128)S(1)} collective-permute-done((f32[64,2048]{1,0:T(8,128)S(1)}, f32[64,2048]{1,0:T(8,128)S(1)}, u32[]{:S(2)}, u32[]{:S(2)}) %collective-permute-start.54) | collective-permute-done | bytes 524320 | tf_op jit(solution)/shard_map/ppermute | solution.py:289
  388.7 9.7 %collective-permute-done.58.refs_15_ = f32[64,2048]{1,0:T(8,128)S(1)} collective-permute-done((f32[64,2048]{1,0:T(8,128)S(1)}, f32[64,2048]{1,0:T(8,128)S(1)}, u32[]{:S(2)}, u32[]{:S(2)}) %collective-permute-start.58) | collective-permute-done | bytes 524320 | tf_op jit(solution)/shard_map/ppermute | solution.py:289
  399.0 9.4 %collective-permute-done.64.refs_21_ = f32[64,2048]{1,0:T(8,128)S(1)} collective-permute-done((f32[64,2048]{1,0:T(8,128)S(1)}, f32[64,2048]{1,0:T(8,128)S(1)}, u32[]{:S(2)}, u32[]{:S(2)}) %collective-permute-start.64) | collective-permute-done | bytes 524320 | tf_op jit(solution)/shard_map/ppermute | solution.py:289
  412.4 10.7 %collective-permute-done.66.refs_23_ = f32[64,2048]{1,0:T(8,128)S(1)} collective-permute-done((f32[64,2048]{1,0:T(8,128)S(1)}, f32[64,2048]{1,0:T(8,128)S(1)}, u32[]{:S(2)}, u32[]{:S(2)}) %collective-permute-start.66) | collective-permute-done | bytes 524320 | tf_op jit(solution)/shard_map/ppermute | solution.py:289
  424.9 9.0 %collective-permute-done.70.refs_27_ = f32[64,2048]{1,0:T(8,128)S(1)} collective-permute-done((f32[64,2048]{1,0:T(8,128)S(1)}, f32[64,2048]{1,0:T(8,128)S(1)}, u32[]{:S(2)}, u32[]{:S(2)}) %collective-permute-start.70) | collective-permute-done | bytes 524320 | tf_op jit(solution)/shard_map/ppermute | solution.py:289
  437.5 11.4 %collective-permute-done.74.refs_31_ = f32[64,2048]{1,0:T(8,128)S(1)} collective-permute-done((f32[64,2048]{1,0:T(8,128)S(1)}, f32[64,2048]{1,0:T(8,128)S(1)}, u32[]{:S(2)}, u32[]{:S(2)}) %collective-permute-start.74) | collective-permute-done | bytes 524320 | tf_op jit(solution)/shard_map/ppermute | solution.py:289
  451.1 91.1 %shard_map.42 = f32[64,2048]{1,0:T(8,128)} custom-call(s32[39]{0:T(128)} %constant.190.clone.refs_0_, f32[64,2048]{1,0:T(8,128)} %copy-done.2, f32[64,2048]{1,0:T(8,128)} %copy-done.14, f32[64,2048]{1,0:T(8,128)} %copy-done.11, f32[64,2048]{1,0:T(8,128)} %copy-done.21, f32[64,2048]{1,0:T(8,128)} %copy-done.10, f32[64,2048]{1,0:T(8,128)} %copy-done.22, ...), custom_call_target="tpu_custom_call" | custom-call | tf_op jit(solution)/shard_map/pallas_call | solution.py:248
  (266 shorter events, 89.1 us)
Async XLA Ops:
  11.3 29.8 %collective-permute-start.30 = (f32[512,512]{1,0:T(8,128)S(1)}, f32[512,512]{1,0:T(8,128)}, u32[]{:S(2)}, u32[]{:S(2)}) collective-permute-start(f32[512,512]{1,0:T(8,128)S(1)} %get-tuple-element.25), channel_id=1, source_target_pairs={{0,8},{1,9},{2,10},{3,11},{4,12},{5,13},{6,14},{7,15},{8,0},{9,1},... | collective-permute-start | bytes 3145736 | tf_op jit(solution)/shard_map/ppermute | solution.py:289
  11.5 29.7 %collective-permute-start.32 = (f32[512,512]{1,0:T(8,128)S(1)}, f32[512,512]{1,0:T(8,128)}, u32[]{:S(2)}, u32[]{:S(2)}) collective-permute-start(f32[512,512]{1,0:T(8,128)S(1)} %get-tuple-element.32.refs_0_), channel_id=1, source_target_pairs={{0,16},{1,17},{2,18},{3,19},{4,20},{5,21},{6,22},{7,23},{8,24},{9,... | collective-permute-start | bytes 3145736 | tf_op jit(solution)/shard_map/ppermute | solution.py:289
  15.0 25.0 %collective-permute-start.9 = (f32[256,512]{1,0:T(8,128)S(1)}, f32[256,512]{1,0:T(8,128)S(1)}, u32[]{:S(2)}, u32[]{:S(2)}) collective-permute-start(f32[256,512]{1,0:T(8,128)S(1)} %maximum_select_fusion.refs_0_), channel_id=1, source_target_pairs={{0,4},{1,5},{2,6},{3,7},{4,0},{5,1},{6,2},{7,3},{8,12},{9,13},{10,... | collective-permute-start | bytes 1572872 | tf_op jit(solution)/shard_map/ppermute | solution.py:289
  37.6 26.1 %collective-permute-start.23 = (f32[512,512]{1,0:T(8,128)S(1)}, f32[512,512]{1,0:T(8,128)}, u32[]{:S(2)}, u32[]{:S(2)}) collective-permute-start(f32[512,512]{1,0:T(8,128)S(1)} %get-tuple-element.26), channel_id=1, source_target_pairs={{0,8},{1,9},{2,10},{3,11},{4,12},{5,13},{6,14},{7,15},{8,0},{9,1},... | collective-permute-start | bytes 3145736 | tf_op jit(solution)/shard_map/ppermute | solution.py:289
  40.0 26.7 %collective-permute-start.25 = (f32[512,512]{1,0:T(8,128)S(1)}, f32[512,512]{1,0:T(8,128)S(1)}, u32[]{:S(2)}, u32[]{:S(2)}) collective-permute-start(f32[512,512]{1,0:T(8,128)S(1)} %get-tuple-element.27.refs_0_), channel_id=1, source_target_pairs={{0,16},{1,17},{2,18},{3,19},{4,20},{5,21},{6,22},{7,23},{8,24},{9,... | collective-permute-start | bytes 3145736 | tf_op jit(solution)/shard_map/ppermute | solution.py:289
  41.1 27.1 %collective-permute-start.22 = (f32[512,512]{1,0:T(8,128)S(1)}, f32[512,512]{1,0:T(8,128)S(1)}, u32[]{:S(2)}, u32[]{:S(2)}) collective-permute-start(f32[512,512]{1,0:T(8,128)S(1)} %get-tuple-element.27.refs_0_), channel_id=1, source_target_pairs={{0,1},{1,0},{2,3},{3,2},{4,5},{5,4},{6,7},{7,6},{8,9},{9,8},{10,11... | collective-permute-start | bytes 3145736 | tf_op jit(solution)/shard_map/ppermute | solution.py:289
  41.1 44.3 %collective-permute-start.16 = (f32[512,512]{1,0:T(8,128)S(1)}, f32[512,512]{1,0:T(8,128)S(1)}, u32[]{:S(2)}, u32[]{:S(2)}) collective-permute-start(f32[512,512]{1,0:T(8,128)S(1)} %get-tuple-element.28), channel_id=1, source_target_pairs={{0,8},{1,9},{2,10},{3,11},{4,12},{5,13},{6,14},{7,15},{8,0},{9,1},... | collective-permute-start | bytes 3145736 | tf_op jit(solution)/shard_map/ppermute | solution.py:289
  44.1 56.9 %collective-permute-start.18 = (f32[512,512]{1,0:T(8,128)S(1)}, f32[512,512]{1,0:T(8,128)S(1)}, u32[]{:S(2)}, u32[]{:S(2)}) collective-permute-start(f32[512,512]{1,0:T(8,128)S(1)} %get-tuple-element.29.refs_0_), channel_id=1, source_target_pairs={{0,16},{1,17},{2,18},{3,19},{4,20},{5,21},{6,22},{7,23},{8,24},{9,... | collective-permute-start | bytes 3145736 | tf_op jit(solution)/shard_map/ppermute | solution.py:289
  63.8 37.2 %collective-permute-start.13 = (f32[256,512]{1,0:T(8,128)S(1)}, f32[256,512]{1,0:T(8,128)S(1)}, u32[]{:S(2)}, u32[]{:S(2)}) collective-permute-start(f32[256,512]{1,0:T(8,128)S(1)} %collective-permute-done.11.refs_4_), channel_id=1, source_target_pairs={{0,4},{1,5},{2,6},{3,7},{4,0},{5,1},{6,2},{7,3},{8,12},{9,13},{10,... | collective-permute-start | bytes 1572872 | tf_op jit(solution)/shard_map/ppermute | solution.py:289
  66.7 66.2 %collective-permute-start.34 = (f32[512,512]{1,0:T(8,128)}, f32[512,512]{1,0:T(8,128)}, u32[]{:S(2)}, u32[]{:S(2)}) collective-permute-start(f32[512,512]{1,0:T(8,128)} %collective-permute-done.30.refs_2_), channel_id=1, source_target_pairs={{0,16},{1,17},{2,18},{3,19},{4,20},{5,21},{6,22},{7,23},{8,24},{9,... | collective-permute-start | bytes 3145736 | tf_op jit(solution)/shard_map/ppermute | solution.py:289
  68.2 42.8 %collective-permute-start.10 = (f32[256,512]{1,0:T(8,128)S(1)}, f32[256,512]{1,0:T(8,128)S(1)}, u32[]{:S(2)}, u32[]{:S(2)}) collective-permute-start(f32[256,512]{1,0:T(8,128)S(1)} %collective-permute-done.8.refs_1_), channel_id=1, source_target_pairs={{0,4},{1,5},{2,6},{3,7},{4,0},{5,1},{6,2},{7,3},{8,12},{9,13},{10,... | collective-permute-start | bytes 1572872 | tf_op jit(solution)/shard_map/ppermute | solution.py:289
  85.4 36.1 %collective-permute-start.12 = (f32[256,512]{1,0:T(8,128)S(1)}, f32[256,512]{1,0:T(8,128)S(1)}, u32[]{:S(2)}, u32[]{:S(2)}) collective-permute-start(f32[256,512]{1,0:T(8,128)S(1)} %collective-permute-done.11.refs_4_), channel_id=1, source_target_pairs={{0,2},{1,3},{2,0},{3,1},{4,6},{5,7},{6,4},{7,5},{8,10},{9,11},{10,... | collective-permute-start | bytes 1572872 | tf_op jit(solution)/shard_map/ppermute | solution.py:289
  101.0 30.2 %collective-permute-start.14 = (f32[256,512]{1,0:T(8,128)S(1)}, f32[256,512]{1,0:T(8,128)S(1)}, u32[]{:S(2)}, u32[]{:S(2)}) collective-permute-start(f32[256,512]{1,0:T(8,128)S(1)} %collective-permute-done.13.refs_6_), channel_id=1, source_target_pairs={{0,2},{1,3},{2,0},{3,1},{4,6},{5,7},{6,4},{7,5},{8,10},{9,11},{10,... | collective-permute-start | bytes 1572872 | tf_op jit(solution)/shard_map/ppermute | solution.py:289
  101.0 36.9 %collective-permute-start.15 = (f32[512,512]{1,0:T(8,128)S(1)}, f32[512,512]{1,0:T(8,128)}, u32[]{:S(2)}, u32[]{:S(2)}) collective-permute-start(f32[512,512]{1,0:T(8,128)S(1)} %get-tuple-element.29.refs_0_), channel_id=1, source_target_pairs={{0,1},{1,0},{2,3},{3,2},{4,5},{5,4},{6,7},{7,6},{8,9},{9,8},{10,11... | collective-permute-start | bytes 3145736 | tf_op jit(solution)/shard_map/ppermute | solution.py:289
  111.0 28.4 %collective-permute-start.31 = (f32[512,512]{1,0:T(8,128)}, f32[512,512]{1,0:T(8,128)}, u32[]{:S(2)}, u32[]{:S(2)}) collective-permute-start(f32[512,512]{1,0:T(8,128)} %collective-permute-done.30.refs_2_), channel_id=1, source_target_pairs={{0,1},{1,0},{2,3},{3,2},{4,5},{5,4},{6,7},{7,6},{8,9},{9,8},{10,11... | collective-permute-start | bytes 3145736 | tf_op jit(solution)/shard_map/ppermute | solution.py:289
  137.9 38.7 %collective-permute-start.1 = (f32[512,512]{1,0:T(8,128)}, f32[512,512]{1,0:T(8,128)}, u32[]{:S(2)}, u32[]{:S(2)}) collective-permute-start(f32[512,512]{1,0:T(8,128)} %get-tuple-element.30), channel_id=1, source_target_pairs={{0,8},{1,9},{2,10},{3,11},{4,12},{5,13},{6,14},{7,15},{8,0},{9,1},... | collective-permute-start | bytes 3145736 | tf_op jit(solution)/shard_map/ppermute | solution.py:289
  139.4 37.6 %collective-permute-start.24 = (f32[512,512]{1,0:T(8,128)}, f32[512,512]{1,0:T(8,128)}, u32[]{:S(2)}, u32[]{:S(2)}) collective-permute-start(f32[512,512]{1,0:T(8,128)} %collective-permute-done.23.refs_2_), channel_id=1, source_target_pairs={{0,1},{1,0},{2,3},{3,2},{4,5},{5,4},{6,7},{7,6},{8,9},{9,8},{10,11... | collective-permute-start | bytes 3145736 | tf_op jit(solution)/shard_map/ppermute | solution.py:289
  139.6 37.6 %collective-permute-start.26 = (f32[512,512]{1,0:T(8,128)}, f32[512,512]{1,0:T(8,128)}, u32[]{:S(2)}, u32[]{:S(2)}) collective-permute-start(f32[512,512]{1,0:T(8,128)} %copy-done.47), channel_id=1, source_target_pairs={{0,1},{1,0},{2,3},{3,2},{4,5},{5,4},{6,7},{7,6},{8,9},{9,8},{10,11... | collective-permute-start | bytes 3145736 | tf_op jit(solution)/shard_map/ppermute | solution.py:289
  176.6 26.1 %collective-permute-start.3 = (f32[512,512]{1,0:T(8,128)S(1)}, f32[512,512]{1,0:T(8,128)S(1)}, u32[]{:S(2)}, u32[]{:S(2)}) collective-permute-start(f32[512,512]{1,0:T(8,128)S(1)} %get-tuple-element.31.refs_0_), channel_id=1, source_target_pairs={{0,16},{1,17},{2,18},{3,19},{4,20},{5,21},{6,22},{7,23},{8,24},{9,... | collective-permute-start | bytes 3145736 | tf_op jit(solution)/shard_map/ppermute | solution.py:289
  177.0 25.7 %collective-permute-start.17 = (f32[512,512]{1,0:T(8,128)}, f32[512,512]{1,0:T(8,128)}, u32[]{:S(2)}, u32[]{:S(2)}) collective-permute-start(f32[512,512]{1,0:T(8,128)} %copy-done.45), channel_id=1, source_target_pairs={{0,1},{1,0},{2,3},{3,2},{4,5},{5,4},{6,7},{7,6},{8,9},{9,8},{10,11... | collective-permute-start | bytes 3145736 | tf_op jit(solution)/shard_map/ppermute | solution.py:289
  177.2 26.0 %collective-permute-start.19 = (f32[512,512]{1,0:T(8,128)}, f32[512,512]{1,0:T(8,128)}, u32[]{:S(2)}, u32[]{:S(2)}) collective-permute-start(f32[512,512]{1,0:T(8,128)} %copy-done.46), channel_id=1, source_target_pairs={{0,1},{1,0},{2,3},{3,2},{4,5},{5,4},{6,7},{7,6},{8,9},{9,8},{10,11... | collective-permute-start | bytes 3145736 | tf_op jit(solution)/shard_map/ppermute | solution.py:289
  178.1 46.6 %collective-permute-start.5 = (f32[512,512]{1,0:T(8,128)}, f32[512,512]{1,0:T(8,128)S(1)}, u32[]{:S(2)}, u32[]{:S(2)}) collective-permute-start(f32[512,512]{1,0:T(8,128)} %collective-permute-done.1.refs_2_), channel_id=1, source_target_pairs={{0,16},{1,17},{2,18},{3,19},{4,20},{5,21},{6,22},{7,23},{8,24},{9,... | collective-permute-start | bytes 3145736 | tf_op jit(solution)/shard_map/ppermute | solution.py:289
  179.6 45.0 %collective-permute-start.21 = (f32[512,512]{1,0:T(8,128)}, f32[512,512]{1,0:T(8,128)}, u32[]{:S(2)}, u32[]{:S(2)}) collective-permute-start(f32[512,512]{1,0:T(8,128)} %collective-permute-done.20.refs_6_), channel_id=1, source_target_pairs={{0,1},{1,0},{2,3},{3,2},{4,5},{5,4},{6,7},{7,6},{8,9},{9,8},{10,11... | collective-permute-start | bytes 3145736 | tf_op jit(solution)/shard_map/ppermute | solution.py:289
  202.7 43.2 %collective-permute-start = (f32[512,512]{1,0:T(8,128)S(1)}, f32[512,512]{1,0:T(8,128)}, u32[]{:S(2)}, u32[]{:S(2)}) collective-permute-start(f32[512,512]{1,0:T(8,128)S(1)} %get-tuple-element.31.refs_0_), channel_id=1, source_target_pairs={{0,1},{1,0},{2,3},{3,2},{4,5},{5,4},{6,7},{7,6},{8,9},{9,8},{10,11... | collective-permute-start | bytes 3145736 | tf_op jit(solution)/shard_map/ppermute | solution.py:289
  202.7 43.2 %collective-permute-start.2 = (f32[512,512]{1,0:T(8,128)}, f32[512,512]{1,0:T(8,128)}, u32[]{:S(2)}, u32[]{:S(2)}) collective-permute-start(f32[512,512]{1,0:T(8,128)} %collective-permute-done.1.refs_2_), channel_id=1, source_target_pairs={{0,1},{1,0},{2,3},{3,2},{4,5},{5,4},{6,7},{7,6},{8,9},{9,8},{10,11... | collective-permute-start | bytes 3145736 | tf_op jit(solution)/shard_map/ppermute | solution.py:289
  203.2 42.7 %collective-permute-start.4 = (f32[512,512]{1,0:T(8,128)S(1)}, f32[512,512]{1,0:T(8,128)}, u32[]{:S(2)}, u32[]{:S(2)}) collective-permute-start(f32[512,512]{1,0:T(8,128)S(1)} %collective-permute-done.3.refs_4_), channel_id=1, source_target_pairs={{0,1},{1,0},{2,3},{3,2},{4,5},{5,4},{6,7},{7,6},{8,9},{9,8},{10,11... | collective-permute-start | bytes 3145736 | tf_op jit(solution)/shard_map/ppermute | solution.py:289
  268.6 25.4 %collective-permute-start.36 = (f32[256,1024]{1,0:T(8,128)S(1)}, f32[256,1024]{1,0:T(8,128)}, u32[]{:S(2)}, u32[]{:S(2)}) collective-permute-start(f32[256,1024]{1,0:T(8,128)S(1)} %slice_bitcast_fusion), channel_id=1, source_target_pairs={{0,8},{1,9},{2,10},{3,11},{4,12},{5,13},{6,14},{7,15},{8,0},{9,1},... | collective-permute-start | bytes 3145736 | tf_op jit(solution)/shard_map/ppermute | solution.py:289
  272.9 25.3 %collective-permute-start.39 = (f32[2,128,1024]{2,1,0:T(8,128)}, f32[2,128,1024]{2,1,0:T(8,128)}, u32[]{:S(2)}, u32[]{:S(2)}) collective-permute-start(f32[2,128,1024]{2,1,0:T(8,128)} %constant_dynamic-slice_fusion.3), channel_id=1, source_target_pairs={{0,2},{1,3},{2,0},{3,1},{4,6},{5,7},{6,4},{7,5},{8,10},{9,11},{10,... | collective-permute-start | bytes 3145736 | tf_op jit(solution)/shard_map/ppermute | solution.py:289
  296.5 26.9 %collective-permute-start.37 = (f32[128,1024]{1,0:T(8,128)}, f32[128,1024]{1,0:T(8,128)}, u32[]{:S(2)}, u32[]{:S(2)}) collective-permute-start(f32[128,1024]{1,0:T(8,128)} %constant_dynamic-slice_fusion.5), channel_id=1, source_target_pairs={{0,2},{1,3},{2,0},{3,1},{4,6},{5,7},{6,4},{7,5},{8,10},{9,11},{10,... | collective-permute-start | bytes 1572872 | tf_op jit(solution)/shard_map/ppermute | solution.py:289
  300.6 26.9 %collective-permute-start.40 = (f32[128,1024]{1,0:T(8,128)S(1)}, f32[128,1024]{1,0:T(8,128)S(1)}, u32[]{:S(2)}, u32[]{:S(2)}) collective-permute-start(f32[128,1024]{1,0:T(8,128)S(1)} %slice_bitcast_fusion.2), channel_id=1, source_target_pairs={{0,8},{1,9},{2,10},{3,11},{4,12},{5,13},{6,14},{7,15},{8,0},{9,1},... | collective-permute-start | bytes 1572872 | tf_op jit(solution)/shard_map/ppermute | solution.py:289
  347.3 25.1 %collective-permute-start.48 = (f32[64,2048]{1,0:T(8,128)S(1)}, f32[64,2048]{1,0:T(8,128)S(1)}, u32[]{:S(2)}, u32[]{:S(2)}) collective-permute-start(f32[64,2048]{1,0:T(8,128)S(1)} %fusion.2.refs_1_), channel_id=1, source_target_pairs={{0,4},{1,5},{2,6},{3,7},{4,0},{5,1},{6,2},{7,3},{8,12},{9,13},{10,... | collective-permute-start | bytes 1572872 | tf_op jit(solution)/shard_map/ppermute | solution.py:289
  347.4 25.1 %collective-permute-start.46 = (f32[64,2048]{1,0:T(8,128)S(1)}, f32[64,2048]{1,0:T(8,128)S(1)}, u32[]{:S(2)}, u32[]{:S(2)}) collective-permute-start(f32[64,2048]{1,0:T(8,128)S(1)} %fusion.2.refs_1_), channel_id=1, source_target_pairs={{0,2},{1,3},{2,0},{3,1},{4,6},{5,7},{6,4},{7,5},{8,10},{9,11},{10,... | collective-permute-start | bytes 1572872 | tf_op jit(solution)/shard_map/ppermute | solution.py:289
  (99 other events, 3014.8 us)
where the time goes:
time: 563 us; the launch traced here: 554 us
  waiting for transfers between devices  283 us (50%)
  Pallas kernels  179 us (32%)
  starting transfers between devices  64.1 us (11%)
  local copies, waits for them, and re-layouts  18.6 us (3%)
  other arithmetic  7.84 us (1%)
    ppermute x79, waiting for transfers between devices, swap(): return lax.ppermute(value, AXES, pairs)  283 us
    pallas_call x1, Pallas kernels, newton(): pl.pallas_call(functools.partial(newton_kernel, last, block, rows, places...  91.1 us
    pallas_call x4, Pallas kernels, moment_chunk(): pl.pallas_call(functools.partial(moment_kernel, first, n_p), grid=(BLOCKS...  83.4 us
    ppermute x79, starting transfers between devices, swap(): return lax.ppermute(value, AXES, pairs)  64.1 us
  transfers between devices with their start and end apart: 79, of which 39 were waited for; matrix products, arithmetic and copies ran while one was open for 3% of the time, Pallas kernels for 12%

commit v1 on v0

--- a/solution.py
+++ b/solution.py
@@ -10,7 +10,8 @@
 
 NS_STEPS = 3
 AXES = ("comp", "samp")
-CHUNKS = 4
+PARTS = (2, 2, 2, 1, 1)
+CHUNKS = len(PARTS)
 BLOCKS = 2
 LANES = 128
 VMEM_BYTES = 60 * 2**20
@@ -306,12 +307,13 @@
     near_half = swap(own_half, comp_bits=1)
 
     half = n_local // 2
-    size = half // CHUNKS
+    unit = half // sum(PARTS)
     chunks = [[None] * n_c for _ in range(CHUNKS)]
     for j, pieces in enumerate(chunks):
-        sent = lax.dynamic_slice_in_dim(samples, (1 - x) * half + j * size, size, 1)
+        size, offset = PARTS[j] * unit, sum(PARTS[:j]) * unit
+        sent = lax.dynamic_slice_in_dim(samples, (1 - x) * half + offset, size, 1)
         pieces[1] = swap(sent, comp_bits=1)
-        pieces[0] = lax.dynamic_slice_in_dim(samples, x * half + j * size, size, 1)
+        pieces[0] = lax.dynamic_slice_in_dim(samples, x * half + offset, size, 1)
         for r in range(2, n_c, 2):
             pieces[r] = swap(pieces[0], comp_bits=r)
         for r in range(2, n_c, 2):

time: 563 us -> 567 us (level)
    pallas_call x4 -> x5, Pallas kernels: 83.4 us -> 88.7 us  [moment_chunk(): pl.pallas_call(functools.partial(moment_kernel, first, n_p), grid=(BLOCKS...]
    ppermute x79 -> x86, starting transfers between devices: 64.1 us -> 61.3 us  [swap(): return lax.ppermute(value, AXES, pairs)]
    ppermute x79 -> x86, waiting for transfers between devices: 283 us -> 284 us  [swap(): return lax.ppermute(value, AXES, pairs)]
  transfers between devices with their start and end apart: 79 -> 86, of which waited for: 39 -> 38; matrix products, arithmetic and copies ran while one was open for 3% -> 3% of each run, Pallas kernels for 12% -> 14%
where the time goes in v1:
time: 567 us; the launch traced here: 559 us
  waiting for transfers between devices  284 us (50%)
  Pallas kernels  184 us (32%)
  starting transfers between devices  61.3 us (11%)
  local copies, waits for them, and re-layouts  20 us (4%)
  other arithmetic  7.84 us (1%)
    ppermute x86, waiting for transfers between devices, swap(): return lax.ppermute(value, AXES, pairs)  284 us
    pallas_call x1, Pallas kernels, newton(): pl.pallas_call(functools.partial(newton_kernel, last, block, rows, places...  90.8 us
    pallas_call x5, Pallas kernels, moment_chunk(): pl.pallas_call(functools.partial(moment_kernel, first, n_p), grid=(BLOCKS...  88.7 us
    ppermute x86, starting transfers between devices, swap(): return lax.ppermute(value, AXES, pairs)  61.3 us
  transfers between devices with their start and end apart: 86, of which 38 were waited for; matrix products, arithmetic and copies ran while one was open for 3% of the time, Pallas kernels for 14%

profile of v1, /device:TPU:0, one launch (start us, length us, event | category | flops | bytes accessed | tf_op | source)
XLA Modules:
  0.0 558.6 jit_solution(11852124535290778857)
XLA Ops:
  10.7 4.6 constant_dynamic-slice_fusion.6
  15.4 6.8 %collective-permute-done.16.refs_2_ = f32[512,256]{1,0:T(8,128)} collective-permute-done((f32[512,256]{1,0:T(8,128)}, f32[512,256]{1,0:T(8,128)}, u32[]{:S(2)}, u32[]{:S(2)}) %collective-permute-start.16) | collective-permute-done | bytes 524320 | tf_op jit(solution)/shard_map/ppermute | solution.py:290
  27.9 5.6 collective-permute-done.1.refs_2_
  33.7 10.9 %collective-permute-done.11.refs_4_ = f32[256,512]{1,0:T(8,128)} collective-permute-done((f32[256,512]{1,0:T(8,128)S(1)}, f32[256,512]{1,0:T(8,128)}, u32[]{:S(2)}, u32[]{:S(2)}) %collective-permute-start.11) | collective-permute-done | bytes 524320 | tf_op jit(solution)/shard_map/ppermute | solution.py:290
  50.1 17.0 %collective-permute-done.37.refs_2_ = f32[512,512]{1,0:T(8,128)} collective-permute-done((f32[512,512]{1,0:T(8,128)S(1)}, f32[512,512]{1,0:T(8,128)}, u32[]{:S(2)}, u32[]{:S(2)}) %collective-permute-start.37) | collective-permute-done | bytes 1048608 | tf_op jit(solution)/shard_map/ppermute | solution.py:290
  70.2 18.7 %collective-permute-done.30.refs_2_ = f32[512,512]{1,0:T(8,128)} collective-permute-done((f32[512,512]{1,0:T(8,128)S(1)}, f32[512,512]{1,0:T(8,128)}, u32[]{:S(2)}, u32[]{:S(2)}) %collective-permute-start.30) | collective-permute-done | bytes 1048608 | tf_op jit(solution)/shard_map/ppermute | solution.py:290
  93.2 12.2 %collective-permute-done.13.refs_6_ = f32[256,512]{1,0:T(8,128)S(1)} collective-permute-done((f32[256,512]{1,0:T(8,128)}, f32[256,512]{1,0:T(8,128)S(1)}, u32[]{:S(2)}, u32[]{:S(2)}) %collective-permute-start.13) | collective-permute-done | bytes 524320 | tf_op jit(solution)/shard_map/ppermute | solution.py:290
  107.4 9.0 %collective-permute-done.10.refs_3_ = f32[256,512]{1,0:T(8,128)S(1)} collective-permute-done((f32[256,512]{1,0:T(8,128)S(1)}, f32[256,512]{1,0:T(8,128)S(1)}, u32[]{:S(2)}, u32[]{:S(2)}) %collective-permute-start.10) | collective-permute-done | bytes 524320 | tf_op jit(solution)/shard_map/ppermute | solution.py:290
  117.2 10.8 %collective-permute-done.14.refs_7_ = f32[256,512]{1,0:T(8,128)S(1)} collective-permute-done((f32[256,512]{1,0:T(8,128)S(1)}, f32[256,512]{1,0:T(8,128)S(1)}, u32[]{:S(2)}, u32[]{:S(2)}) %collective-permute-start.14) | collective-permute-done | bytes 524320 | tf_op jit(solution)/shard_map/ppermute | solution.py:290
  129.0 4.9 shard_map.37
  135.7 18.7 %collective-permute-done.34.refs_6_ = f32[512,512]{1,0:T(8,128)} collective-permute-done((f32[512,512]{1,0:T(8,128)}, f32[512,512]{1,0:T(8,128)}, u32[]{:S(2)}, u32[]{:S(2)}) %collective-permute-start.34) | collective-permute-done | bytes 1048608 | tf_op jit(solution)/shard_map/ppermute | solution.py:290
  154.9 19.9 %shard_map.38 = (f32[512,2048]{1,0:T(8,128)}, f32[512,128]{1,0:T(8,128)}) custom-call(f32[512,512]{1,0:T(8,128)} %copy-done.5, f32[512,512]{1,0:T(8,128)} %copy-done.47, f32[512,512]{1,0:T(8,128)} %collective-permute-done.37.refs_2_, f32[512,512]{1,0:T(8,128)} %collective-permute-done.38.refs_3_, f32[512,512]{1,0:T(8,128)} %collective-permute-done.39.refs_4_, ...), custom_call_target="tpu_custom_call" | custom-call | flops 12884901888 | bytes 20971520 | tf_op jit(solution)/shard_map/pallas_call | solution.py:104
  177.6 21.8 %collective-permute-done.27.refs_6_ = f32[512,512]{1,0:T(8,128)} collective-permute-done((f32[512,512]{1,0:T(8,128)}, f32[512,512]{1,0:T(8,128)}, u32[]{:S(2)}, u32[]{:S(2)}) %collective-permute-start.27) | collective-permute-done | bytes 1048608 | tf_op jit(solution)/shard_map/ppermute | solution.py:290
  199.9 21.5 %shard_map.39 = (f32[512,2048]{1,0:T(8,128)}, f32[512,128]{1,0:T(8,128)}) custom-call(f32[512,512]{1,0:T(8,128)} %copy-done.4, f32[512,512]{1,0:T(8,128)} %copy-done.46, f32[512,512]{1,0:T(8,128)} %collective-permute-done.30.refs_2_, f32[512,512]{1,0:T(8,128)} %copy-done.49, f32[512,512]{1,0:T(8,128)} %copy-done.45, ...), custom_call_target="tpu_custom_call", output_to_operand_aliasing={{0}: (10, {}), {1}: (11, {})} | custom-call | flops 12884901888 | bytes 20971520 | tf_op jit(solution)/shard_map/pallas_call | solution.py:104
  224.0 21.1 %shard_map.40 = (f32[512,2048]{1,0:T(8,128)}, f32[512,128]{1,0:T(8,128)}) custom-call(f32[512,512]{1,0:T(8,128)} %copy-done.3, f32[512,512]{1,0:T(8,128)} %copy-done.48, f32[512,512]{1,0:T(8,128)} %collective-permute-done.23.refs_2_, f32[512,512]{1,0:T(8,128)} %collective-permute-done.24.refs_3_, ...), custom_call_target="tpu_custom_call", output_to_operand_aliasing={{0}: (10, {}), {1}: (11, {})} | custom-call | flops 12884901888 | bytes 20971520 | tf_op jit(solution)/shard_map/pallas_call | solution.py:104
  246.5 13.1 %shard_map.41 = (f32[512,2048]{1,0:T(8,128)}, f32[512,128]{1,0:T(8,128)}) custom-call(f32[512,256]{1,0:T(8,128)} %copy-done.40, f32[512,256]{1,0:T(8,128)} %collective-permute-done.15.refs_1_, f32[512,256]{1,0:T(8,128)} %collective-permute-done.16.refs_2_, f32[512,256]{1,0:T(8,128)} %copy-done.53, ...), custom_call_target="tpu_custom_call", output_to_operand_aliasing={{0}: (10, {}), {1}: (11, {})} | custom-call | flops 6442450944 | bytes 16777216 | tf_op jit(solution)/shard_map/pallas_call | solution.py:104
  260.6 13.2 %shard_map.42 = (f32[512,2048]{1,0:T(8,128)}, f32[512,128]{1,0:T(8,128)}) custom-call(f32[512,256]{1,0:T(8,128)} %get-tuple-element.38.refs_0_, f32[512,256]{1,0:T(8,128)} %copy-done.54, f32[512,256]{1,0:T(8,128)} %collective-permute-done.1.refs_2_, f32[512,256]{1,0:T(8,128)} %copy-done.55, ...), custom_call_target="tpu_custom_call", output_to_operand_aliasing={{0}: (10, {}), {1}: (11, {})} | custom-call | flops 6442450944 | bytes 16777216 | tf_op jit(solution)/shard_map/pallas_call | solution.py:104
  279.5 21.3 %collective-permute-done.43 = f32[256,1024]{1,0:T(8,128)} collective-permute-done((f32[256,1024]{1,0:T(8,128)S(1)}, f32[256,1024]{1,0:T(8,128)}, u32[]{:S(2)}, u32[]{:S(2)}) %collective-permute-start.43) | collective-permute-done | bytes 1048608 | tf_op jit(solution)/shard_map/ppermute | solution.py:290
  309.7 10.9 %collective-permute-done.49 = f32[2,256]{1,0:T(2,128)S(1)} collective-permute-done((f32[2,256]{1,0:T(2,128)S(1)}, f32[2,256]{1,0:T(2,128)S(1)}, u32[]{:S(2)}, u32[]{:S(2)}) %collective-permute-start.49) | collective-permute-done | bytes 2080 | tf_op jit(solution)/shard_map/ppermute | solution.py:290
  321.3 3.0 collective-permute-done.50
  334.2 13.4 %collective-permute-done.45 = f32[64,1024]{1,0:T(8,128)S(1)} collective-permute-done((f32[64,1024]{1,0:T(8,128)S(1)}, f32[64,1024]{1,0:T(8,128)S(1)}, u32[]{:S(2)}, u32[]{:S(2)}) %collective-permute-start.45) | collective-permute-done | bytes 262176 | tf_op jit(solution)/shard_map/ppermute | solution.py:290
  347.6 4.5 collective-permute-done.48
  352.3 3.6 collective-permute-start.53
  356.9 20.4 %collective-permute-done.55.refs_5_ = f32[64,2048]{1,0:T(8,128)S(1)} collective-permute-done((f32[64,2048]{1,0:T(8,128)S(1)}, f32[64,2048]{1,0:T(8,128)S(1)}, u32[]{:S(2)}, u32[]{:S(2)}) %collective-permute-start.55) | collective-permute-done | bytes 524320 | tf_op jit(solution)/shard_map/ppermute | solution.py:290
  381.5 8.4 %collective-permute-done.61.refs_11_ = f32[64,2048]{1,0:T(8,128)S(1)} collective-permute-done((f32[64,2048]{1,0:T(8,128)S(1)}, f32[64,2048]{1,0:T(8,128)S(1)}, u32[]{:S(2)}, u32[]{:S(2)}) %collective-permute-start.61) | collective-permute-done | bytes 524320 | tf_op jit(solution)/shard_map/ppermute | solution.py:290
  393.5 10.0 %collective-permute-done.65.refs_15_ = f32[64,2048]{1,0:T(8,128)S(1)} collective-permute-done((f32[64,2048]{1,0:T(8,128)S(1)}, f32[64,2048]{1,0:T(8,128)S(1)}, u32[]{:S(2)}, u32[]{:S(2)}) %collective-permute-start.65) | collective-permute-done | bytes 524320 | tf_op jit(solution)/shard_map/ppermute | solution.py:290
  404.0 9.1 %collective-permute-done.71.refs_21_ = f32[64,2048]{1,0:T(8,128)S(1)} collective-permute-done((f32[64,2048]{1,0:T(8,128)S(1)}, f32[64,2048]{1,0:T(8,128)S(1)}, u32[]{:S(2)}, u32[]{:S(2)}) %collective-permute-start.71) | collective-permute-done | bytes 524320 | tf_op jit(solution)/shard_map/ppermute | solution.py:290
  417.2 10.7 %collective-permute-done.73.refs_23_ = f32[64,2048]{1,0:T(8,128)S(1)} collective-permute-done((f32[64,2048]{1,0:T(8,128)S(1)}, f32[64,2048]{1,0:T(8,128)S(1)}, u32[]{:S(2)}, u32[]{:S(2)}) %collective-permute-start.73) | collective-permute-done | bytes 524320 | tf_op jit(solution)/shard_map/ppermute | solution.py:290
  429.6 9.0 %collective-permute-done.77.refs_27_ = f32[64,2048]{1,0:T(8,128)S(1)} collective-permute-done((f32[64,2048]{1,0:T(8,128)S(1)}, f32[64,2048]{1,0:T(8,128)S(1)}, u32[]{:S(2)}, u32[]{:S(2)}) %collective-permute-start.77) | collective-permute-done | bytes 524320 | tf_op jit(solution)/shard_map/ppermute | solution.py:290
  442.2 11.4 %collective-permute-done.81.refs_31_ = f32[64,2048]{1,0:T(8,128)S(1)} collective-permute-done((f32[64,2048]{1,0:T(8,128)S(1)}, f32[64,2048]{1,0:T(8,128)S(1)}, u32[]{:S(2)}, u32[]{:S(2)}) %collective-permute-start.81) | collective-permute-done | bytes 524320 | tf_op jit(solution)/shard_map/ppermute | solution.py:290
  455.8 90.8 %shard_map.43 = f32[64,2048]{1,0:T(8,128)} custom-call(s32[39]{0:T(128)} %constant.195.clone.refs_0_, f32[64,2048]{1,0:T(8,128)} %copy-done.2, f32[64,2048]{1,0:T(8,128)} %copy-done.13, f32[64,2048]{1,0:T(8,128)} %copy-done.10, f32[64,2048]{1,0:T(8,128)} %copy-done.20, f32[64,2048]{1,0:T(8,128)} %copy-done.9, f32[64,2048]{1,0:T(8,128)} %copy-done.21, ...), custom_call_target="tpu_custom_call" | custom-call | tf_op jit(solution)/shard_map/pallas_call | solution.py:249
  551.2 2.9 collective-permute-done.83
  (290 shorter events, 98.5 us)
Async XLA Ops:
  8.6 24.9 %collective-permute-start.1 = (f32[512,256]{1,0:T(8,128)}, f32[512,256]{1,0:T(8,128)}, u32[]{:S(2)}, u32[]{:S(2)}) collective-permute-start(f32[512,256]{1,0:T(8,128)} %get-tuple-element.37), channel_id=1, source_target_pairs={{0,8},{1,9},{2,10},{3,11},{4,12},{5,13},{6,14},{7,15},{8,0},{9,1},... | collective-permute-start | bytes 1572872 | tf_op jit(solution)/shard_map/ppermute | solution.py:290
  9.2 35.5 %collective-permute-start.11 = (f32[256,512]{1,0:T(8,128)S(1)}, f32[256,512]{1,0:T(8,128)}, u32[]{:S(2)}, u32[]{:S(2)}) collective-permute-start(f32[256,512]{1,0:T(8,128)S(1)} %maximum_select_fusion.refs_0_), channel_id=1, source_target_pairs={{0,8},{1,9},{2,10},{3,11},{4,12},{5,13},{6,14},{7,15},{8,0},{9,1},... | collective-permute-start | bytes 1572872 | tf_op jit(solution)/shard_map/ppermute | solution.py:290
  22.2 44.9 %collective-permute-start.37 = (f32[512,512]{1,0:T(8,128)S(1)}, f32[512,512]{1,0:T(8,128)}, u32[]{:S(2)}, u32[]{:S(2)}) collective-permute-start(f32[512,512]{1,0:T(8,128)S(1)} %get-tuple-element.29), channel_id=1, source_target_pairs={{0,8},{1,9},{2,10},{3,11},{4,12},{5,13},{6,14},{7,15},{8,0},{9,1},... | collective-permute-start | bytes 3145736 | tf_op jit(solution)/shard_map/ppermute | solution.py:290
  25.3 24.3 %collective-permute-start.9 = (f32[256,512]{1,0:T(8,128)S(1)}, f32[256,512]{1,0:T(8,128)S(1)}, u32[]{:S(2)}, u32[]{:S(2)}) collective-permute-start(f32[256,512]{1,0:T(8,128)S(1)} %maximum_select_fusion.refs_0_), channel_id=1, source_target_pairs={{0,4},{1,5},{2,6},{3,7},{4,0},{5,1},{6,2},{7,3},{8,12},{9,13},{10,... | collective-permute-start | bytes 1572872 | tf_op jit(solution)/shard_map/ppermute | solution.py:290
  33.4 33.7 %collective-permute-start.39 = (f32[512,512]{1,0:T(8,128)S(1)}, f32[512,512]{1,0:T(8,128)}, u32[]{:S(2)}, u32[]{:S(2)}) collective-permute-start(f32[512,512]{1,0:T(8,128)S(1)} %get-tuple-element.34.refs_0_), channel_id=1, source_target_pairs={{0,16},{1,17},{2,18},{3,19},{4,20},{5,21},{6,22},{7,23},{8,24},{9,... | collective-permute-start | bytes 3145736 | tf_op jit(solution)/shard_map/ppermute | solution.py:290
  44.7 25.1 %collective-permute-start.36 = (f32[512,512]{1,0:T(8,128)S(1)}, f32[512,512]{1,0:T(8,128)S(1)}, u32[]{:S(2)}, u32[]{:S(2)}) collective-permute-start(f32[512,512]{1,0:T(8,128)S(1)} %get-tuple-element.34.refs_0_), channel_id=1, source_target_pairs={{0,1},{1,0},{2,3},{3,2},{4,5},{5,4},{6,7},{7,6},{8,9},{9,8},{10,11... | collective-permute-start | bytes 3145736 | tf_op jit(solution)/shard_map/ppermute | solution.py:290
  47.2 41.8 %collective-permute-start.30 = (f32[512,512]{1,0:T(8,128)S(1)}, f32[512,512]{1,0:T(8,128)}, u32[]{:S(2)}, u32[]{:S(2)}) collective-permute-start(f32[512,512]{1,0:T(8,128)S(1)} %get-tuple-element.30), channel_id=1, source_target_pairs={{0,8},{1,9},{2,10},{3,11},{4,12},{5,13},{6,14},{7,15},{8,0},{9,1},... | collective-permute-start | bytes 3145736 | tf_op jit(solution)/shard_map/ppermute | solution.py:290
  49.6 42.0 %collective-permute-start.32 = (f32[512,512]{1,0:T(8,128)S(1)}, f32[512,512]{1,0:T(8,128)S(1)}, u32[]{:S(2)}, u32[]{:S(2)}) collective-permute-start(f32[512,512]{1,0:T(8,128)S(1)} %get-tuple-element.31.refs_0_), channel_id=1, source_target_pairs={{0,16},{1,17},{2,18},{3,19},{4,20},{5,21},{6,22},{7,23},{8,24},{9,... | collective-permute-start | bytes 3145736 | tf_op jit(solution)/shard_map/ppermute | solution.py:290
  67.1 38.7 %collective-permute-start.29 = (f32[512,512]{1,0:T(8,128)S(1)}, f32[512,512]{1,0:T(8,128)S(1)}, u32[]{:S(2)}, u32[]{:S(2)}) collective-permute-start(f32[512,512]{1,0:T(8,128)S(1)} %get-tuple-element.31.refs_0_), channel_id=1, source_target_pairs={{0,1},{1,0},{2,3},{3,2},{4,5},{5,4},{6,7},{7,6},{8,9},{9,8},{10,11... | collective-permute-start | bytes 3145736 | tf_op jit(solution)/shard_map/ppermute | solution.py:290
  67.1 38.2 %collective-permute-start.13 = (f32[256,512]{1,0:T(8,128)}, f32[256,512]{1,0:T(8,128)S(1)}, u32[]{:S(2)}, u32[]{:S(2)}) collective-permute-start(f32[256,512]{1,0:T(8,128)} %collective-permute-done.11.refs_4_), channel_id=1, source_target_pairs={{0,4},{1,5},{2,6},{3,7},{4,0},{5,1},{6,2},{7,3},{8,12},{9,13},{10,... | collective-permute-start | bytes 1572872 | tf_op jit(solution)/shard_map/ppermute | solution.py:290
  69.7 59.2 %collective-permute-start.41 = (f32[512,512]{1,0:T(8,128)}, f32[512,512]{1,0:T(8,128)}, u32[]{:S(2)}, u32[]{:S(2)}) collective-permute-start(f32[512,512]{1,0:T(8,128)} %collective-permute-done.37.refs_2_), channel_id=1, source_target_pairs={{0,16},{1,17},{2,18},{3,19},{4,20},{5,21},{6,22},{7,23},{8,24},{9,... | collective-permute-start | bytes 3145736 | tf_op jit(solution)/shard_map/ppermute | solution.py:290
  89.0 27.4 %collective-permute-start.10 = (f32[256,512]{1,0:T(8,128)S(1)}, f32[256,512]{1,0:T(8,128)S(1)}, u32[]{:S(2)}, u32[]{:S(2)}) collective-permute-start(f32[256,512]{1,0:T(8,128)S(1)} %collective-permute-done.8.refs_1_), channel_id=1, source_target_pairs={{0,4},{1,5},{2,6},{3,7},{4,0},{5,1},{6,2},{7,3},{8,12},{9,13},{10,... | collective-permute-start | bytes 1572872 | tf_op jit(solution)/shard_map/ppermute | solution.py:290
  91.6 25.6 %collective-permute-start.12 = (f32[256,512]{1,0:T(8,128)}, f32[256,512]{1,0:T(8,128)S(1)}, u32[]{:S(2)}, u32[]{:S(2)}) collective-permute-start(f32[256,512]{1,0:T(8,128)} %collective-permute-done.11.refs_4_), channel_id=1, source_target_pairs={{0,2},{1,3},{2,0},{3,1},{4,6},{5,7},{6,4},{7,5},{8,10},{9,11},{10,... | collective-permute-start | bytes 1572872 | tf_op jit(solution)/shard_map/ppermute | solution.py:290
  105.9 28.1 %collective-permute-start.23 = (f32[512,512]{1,0:T(8,128)}, f32[512,512]{1,0:T(8,128)}, u32[]{:S(2)}, u32[]{:S(2)}) collective-permute-start(f32[512,512]{1,0:T(8,128)} %get-tuple-element.32), channel_id=1, source_target_pairs={{0,8},{1,9},{2,10},{3,11},{4,12},{5,13},{6,14},{7,15},{8,0},{9,1},... | collective-permute-start | bytes 3145736 | tf_op jit(solution)/shard_map/ppermute | solution.py:290
  128.0 26.3 %collective-permute-start.34 = (f32[512,512]{1,0:T(8,128)}, f32[512,512]{1,0:T(8,128)}, u32[]{:S(2)}, u32[]{:S(2)}) collective-permute-start(f32[512,512]{1,0:T(8,128)} %collective-permute-done.30.refs_2_), channel_id=1, source_target_pairs={{0,16},{1,17},{2,18},{3,19},{4,20},{5,21},{6,22},{7,23},{8,24},{9,... | collective-permute-start | bytes 3145736 | tf_op jit(solution)/shard_map/ppermute | solution.py:290
  128.9 25.9 %collective-permute-start.42 = (f32[512,512]{1,0:T(8,128)}, f32[512,512]{1,0:T(8,128)}, u32[]{:S(2)}, u32[]{:S(2)}) collective-permute-start(f32[512,512]{1,0:T(8,128)} %collective-permute-done.41.refs_6_), channel_id=1, source_target_pairs={{0,1},{1,0},{2,3},{3,2},{4,5},{5,4},{6,7},{7,6},{8,9},{9,8},{10,11... | collective-permute-start | bytes 3145736 | tf_op jit(solution)/shard_map/ppermute | solution.py:290
  134.0 42.9 %collective-permute-start.25 = (f32[512,512]{1,0:T(8,128)S(1)}, f32[512,512]{1,0:T(8,128)}, u32[]{:S(2)}, u32[]{:S(2)}) collective-permute-start(f32[512,512]{1,0:T(8,128)S(1)} %get-tuple-element.33.refs_0_), channel_id=1, source_target_pairs={{0,16},{1,17},{2,18},{3,19},{4,20},{5,21},{6,22},{7,23},{8,24},{9,... | collective-permute-start | bytes 3145736 | tf_op jit(solution)/shard_map/ppermute | solution.py:290
  135.2 41.7 %collective-permute-start.31 = (f32[512,512]{1,0:T(8,128)}, f32[512,512]{1,0:T(8,128)S(1)}, u32[]{:S(2)}, u32[]{:S(2)}) collective-permute-start(f32[512,512]{1,0:T(8,128)} %collective-permute-done.30.refs_2_), channel_id=1, source_target_pairs={{0,1},{1,0},{2,3},{3,2},{4,5},{5,4},{6,7},{7,6},{8,9},{9,8},{10,11... | collective-permute-start | bytes 3145736 | tf_op jit(solution)/shard_map/ppermute | solution.py:290
  135.4 42.0 %collective-permute-start.33 = (f32[512,512]{1,0:T(8,128)}, f32[512,512]{1,0:T(8,128)}, u32[]{:S(2)}, u32[]{:S(2)}) collective-permute-start(f32[512,512]{1,0:T(8,128)} %copy-done.45), channel_id=1, source_target_pairs={{0,1},{1,0},{2,3},{3,2},{4,5},{5,4},{6,7},{7,6},{8,9},{9,8},{10,11... | collective-permute-start | bytes 3145736 | tf_op jit(solution)/shard_map/ppermute | solution.py:290
  154.4 44.9 %collective-permute-start.27 = (f32[512,512]{1,0:T(8,128)}, f32[512,512]{1,0:T(8,128)}, u32[]{:S(2)}, u32[]{:S(2)}) collective-permute-start(f32[512,512]{1,0:T(8,128)} %collective-permute-done.23.refs_2_), channel_id=1, source_target_pairs={{0,16},{1,17},{2,18},{3,19},{4,20},{5,21},{6,22},{7,23},{8,24},{9,... | collective-permute-start | bytes 3145736 | tf_op jit(solution)/shard_map/ppermute | solution.py:290
  154.8 44.5 %collective-permute-start.35 = (f32[512,512]{1,0:T(8,128)}, f32[512,512]{1,0:T(8,128)}, u32[]{:S(2)}, u32[]{:S(2)}) collective-permute-start(f32[512,512]{1,0:T(8,128)} %collective-permute-done.34.refs_6_), channel_id=1, source_target_pairs={{0,1},{1,0},{2,3},{3,2},{4,5},{5,4},{6,7},{7,6},{8,9},{9,8},{10,11... | collective-permute-start | bytes 3145736 | tf_op jit(solution)/shard_map/ppermute | solution.py:290
  176.9 44.5 %collective-permute-start.22 = (f32[512,512]{1,0:T(8,128)S(1)}, f32[512,512]{1,0:T(8,128)S(1)}, u32[]{:S(2)}, u32[]{:S(2)}) collective-permute-start(f32[512,512]{1,0:T(8,128)S(1)} %get-tuple-element.33.refs_0_), channel_id=1, source_target_pairs={{0,1},{1,0},{2,3},{3,2},{4,5},{5,4},{6,7},{7,6},{8,9},{9,8},{10,11... | collective-permute-start | bytes 3145736 | tf_op jit(solution)/shard_map/ppermute | solution.py:290
  176.9 45.0 %collective-permute-start.20 = (f32[512,256]{1,0:T(8,128)}, f32[512,256]{1,0:T(8,128)S(1)}, u32[]{:S(2)}, u32[]{:S(2)}) collective-permute-start(f32[512,256]{1,0:T(8,128)} %collective-permute-done.16.refs_2_), channel_id=1, source_target_pairs={{0,16},{1,17},{2,18},{3,19},{4,20},{5,21},{6,22},{7,23},{8,24},{9,... | collective-permute-start | bytes 1572872 | tf_op jit(solution)/shard_map/ppermute | solution.py:290
  177.4 44.5 %collective-permute-start.24 = (f32[512,512]{1,0:T(8,128)}, f32[512,512]{1,0:T(8,128)}, u32[]{:S(2)}, u32[]{:S(2)}) collective-permute-start(f32[512,512]{1,0:T(8,128)} %collective-permute-done.23.refs_2_), channel_id=1, source_target_pairs={{0,1},{1,0},{2,3},{3,2},{4,5},{5,4},{6,7},{7,6},{8,9},{9,8},{10,11... | collective-permute-start | bytes 3145736 | tf_op jit(solution)/shard_map/ppermute | solution.py:290
  199.3 24.6 %collective-permute-start.28 = (f32[512,512]{1,0:T(8,128)}, f32[512,512]{1,0:T(8,128)}, u32[]{:S(2)}, u32[]{:S(2)}) collective-permute-start(f32[512,512]{1,0:T(8,128)} %collective-permute-done.27.refs_6_), channel_id=1, source_target_pairs={{0,1},{1,0},{2,3},{3,2},{4,5},{5,4},{6,7},{7,6},{8,9},{9,8},{10,11... | collective-permute-start | bytes 3145736 | tf_op jit(solution)/shard_map/ppermute | solution.py:290
  275.1 25.7 %collective-permute-start.43 = (f32[256,1024]{1,0:T(8,128)S(1)}, f32[256,1024]{1,0:T(8,128)}, u32[]{:S(2)}, u32[]{:S(2)}) collective-permute-start(f32[256,1024]{1,0:T(8,128)S(1)} %slice_bitcast_fusion), channel_id=1, source_target_pairs={{0,8},{1,9},{2,10},{3,11},{4,12},{5,13},{6,14},{7,15},{8,0},{9,1},... | collective-permute-start | bytes 3145736 | tf_op jit(solution)/shard_map/ppermute | solution.py:290
  279.5 25.5 %collective-permute-start.46 = (f32[2,128,1024]{2,1,0:T(8,128)}, f32[2,128,1024]{2,1,0:T(8,128)}, u32[]{:S(2)}, u32[]{:S(2)}) collective-permute-start(f32[2,128,1024]{2,1,0:T(8,128)} %constant_dynamic-slice_fusion.3), channel_id=1, source_target_pairs={{0,2},{1,3},{2,0},{3,1},{4,6},{5,7},{6,4},{7,5},{8,10},{9,11},{10,... | collective-permute-start | bytes 3145736 | tf_op jit(solution)/shard_map/ppermute | solution.py:290
  303.3 25.5 %collective-permute-start.44 = (f32[128,1024]{1,0:T(8,128)}, f32[128,1024]{1,0:T(8,128)}, u32[]{:S(2)}, u32[]{:S(2)}) collective-permute-start(f32[128,1024]{1,0:T(8,128)} %constant_dynamic-slice_fusion.5), channel_id=1, source_target_pairs={{0,2},{1,3},{2,0},{3,1},{4,6},{5,7},{6,4},{7,5},{8,10},{9,11},{10,... | collective-permute-start | bytes 1572872 | tf_op jit(solution)/shard_map/ppermute | solution.py:290
  307.4 24.7 %collective-permute-start.47 = (f32[128,1024]{1,0:T(8,128)S(1)}, f32[128,1024]{1,0:T(8,128)S(1)}, u32[]{:S(2)}, u32[]{:S(2)}) collective-permute-start(f32[128,1024]{1,0:T(8,128)S(1)} %slice_bitcast_fusion.2), channel_id=1, source_target_pairs={{0,8},{1,9},{2,10},{3,11},{4,12},{5,13},{6,14},{7,15},{8,0},{9,1},... | collective-permute-start | bytes 1572872 | tf_op jit(solution)/shard_map/ppermute | solution.py:290
  352.2 25.1 %collective-permute-start.55 = (f32[64,2048]{1,0:T(8,128)S(1)}, f32[64,2048]{1,0:T(8,128)S(1)}, u32[]{:S(2)}, u32[]{:S(2)}) collective-permute-start(f32[64,2048]{1,0:T(8,128)S(1)} %fusion.2.refs_1_), channel_id=1, source_target_pairs={{0,4},{1,5},{2,6},{3,7},{4,0},{5,1},{6,2},{7,3},{8,12},{9,13},{10,... | collective-permute-start | bytes 1572872 | tf_op jit(solution)/shard_map/ppermute | solution.py:290
  352.3 25.1 %collective-permute-start.53 = (f32[64,2048]{1,0:T(8,128)S(1)}, f32[64,2048]{1,0:T(8,128)S(1)}, u32[]{:S(2)}, u32[]{:S(2)}) collective-permute-start(f32[64,2048]{1,0:T(8,128)S(1)} %fusion.2.refs_1_), channel_id=1, source_target_pairs={{0,2},{1,3},{2,0},{3,1},{4,6},{5,7},{6,4},{7,5},{8,10},{9,11},{10,... | collective-permute-start | bytes 1572872 | tf_op jit(solution)/shard_map/ppermute | solution.py:290
  379.2 24.2 %collective-permute-start.65 = (f32[64,2048]{1,0:T(8,128)S(1)}, f32[64,2048]{1,0:T(8,128)S(1)}, u32[]{:S(2)}, u32[]{:S(2)}) collective-permute-start(f32[64,2048]{1,0:T(8,128)S(1)} %collective-permute-done.55.refs_5_), channel_id=1, source_target_pairs={{0,8},{1,9},{2,10},{3,11},{4,12},{5,13},{6,14},{7,15},{8,0},{9,1},... | collective-permute-start | bytes 1572872 | tf_op jit(solution)/shard_map/ppermute | solution.py:290
  (110 other events, 2782.3 us)

commit v2 on v1

--- a/solution.py
+++ b/solution.py
@@ -12,7 +12,7 @@
 AXES = ("comp", "samp")
 PARTS = (2, 2, 2, 1, 1)
 CHUNKS = len(PARTS)
-BLOCKS = 2
+BLOCKS = 4
 LANES = 128
 VMEM_BYTES = 60 * 2**20
 f32, bf16 = jnp.float32, jnp.bfloat16
@@ -177,18 +177,21 @@
             bit *= 2
         start = r * rows + start
 
-        @pl.loop(0, size // 16)
+        part_cols = order // 4
+
+        @pl.loop(0, size // 16 * 4)
         def _(q):
-            here = pl.ds(pl.multiple_of(start + q * 16, 16), 16)
-            v = stage[i % slots, pl.ds(pl.multiple_of(q * 16, 16), 16), :]
+            row, cols = q // 4 * 16, pl.ds(pl.multiple_of(q % 4 * part_cols, part_cols), part_cols)
+            here = pl.ds(pl.multiple_of(start + row, 16), 16)
+            v = stage[i % slots, pl.ds(pl.multiple_of(row, 16), 16), cols]
             part = v * v
             total = part[:, :LANES]
-            for t in range(1, order // LANES):
+            for t in range(1, part_cols // LANES):
                 total = total + part[:, t * LANES : (t + 1) * LANES]
             squares[...] += total
             hi, lo = split(v)
-            uh[here, :] = hi
-            ul[here, :] = lo
+            uh[here, cols] = hi
+            ul[here, cols] = lo
 
     @pl.loop(0, order // block)
     def _(b):

time: 567 us -> 590 us (1.041)
  Pallas kernels: 184 us -> 222 us
  waiting for transfers between devices: 284 us -> 272 us
    pallas_call x5, Pallas kernels: 88.7 us -> 124 us  [moment_chunk(): pl.pallas_call(functools.partial(moment_kernel, first, n_p), grid=(BLOCKS...]
    ppermute x86, waiting for transfers between devices: 284 us -> 272 us  [swap(): return lax.ppermute(value, AXES, pairs)]
  transfers between devices with their start and end apart: 86 -> 86, of which waited for: 38 -> 35; matrix products, arithmetic and copies ran while one was open for 3% -> 3% of each run, Pallas kernels for 14% -> 19%
where the time goes in v2:
time: 590 us; the launch traced here: 586 us
  waiting for transfers between devices  272 us (46%)
  Pallas kernels  222 us (38%)
  starting transfers between devices  62.7 us (11%)
  local copies, waits for them, and re-layouts  20.1 us (3%)
  other arithmetic  7.84 us (1%)
    ppermute x86, waiting for transfers between devices, swap(): return lax.ppermute(value, AXES, pairs)  272 us
    pallas_call x5, Pallas kernels, moment_chunk(): pl.pallas_call(functools.partial(moment_kernel, first, n_p), grid=(BLOCKS...  124 us
    pallas_call x1, Pallas kernels, newton(): pl.pallas_call(functools.partial(newton_kernel, last, block, rows, places...  93 us
    ppermute x86, starting transfers between devices, swap(): return lax.ppermute(value, AXES, pairs)  62.7 us
  transfers between devices with their start and end apart: 86, of which 35 were waited for; matrix products, arithmetic and copies ran while one was open for 3% of the time, Pallas kernels for 19%

profile of v2, /device:TPU:0, one launch (start us, length us, event | category | flops | bytes accessed | tf_op | source)
XLA Modules:
  0.0 585.9 jit_solution(16945042601540789078)
XLA Ops:
  10.7 4.6 constant_dynamic-slice_fusion.6
  15.4 6.8 %collective-permute-done.16.refs_2_ = f32[512,256]{1,0:T(8,128)} collective-permute-done((f32[512,256]{1,0:T(8,128)}, f32[512,256]{1,0:T(8,128)}, u32[]{:S(2)}, u32[]{:S(2)}) %collective-permute-start.16) | collective-permute-done | bytes 524320 | tf_op jit(solution)/shard_map/ppermute | solution.py:293
  27.9 5.6 collective-permute-done.1.refs_2_
  33.7 10.9 %collective-permute-done.11.refs_4_ = f32[256,512]{1,0:T(8,128)} collective-permute-done((f32[256,512]{1,0:T(8,128)S(1)}, f32[256,512]{1,0:T(8,128)}, u32[]{:S(2)}, u32[]{:S(2)}) %collective-permute-start.11) | collective-permute-done | bytes 524320 | tf_op jit(solution)/shard_map/ppermute | solution.py:293
  50.1 17.0 %collective-permute-done.37.refs_2_ = f32[512,512]{1,0:T(8,128)} collective-permute-done((f32[512,512]{1,0:T(8,128)S(1)}, f32[512,512]{1,0:T(8,128)}, u32[]{:S(2)}, u32[]{:S(2)}) %collective-permute-start.37) | collective-permute-done | bytes 1048608 | tf_op jit(solution)/shard_map/ppermute | solution.py:293
  70.2 18.7 %collective-permute-done.30.refs_2_ = f32[512,512]{1,0:T(8,128)} collective-permute-done((f32[512,512]{1,0:T(8,128)S(1)}, f32[512,512]{1,0:T(8,128)}, u32[]{:S(2)}, u32[]{:S(2)}) %collective-permute-start.30) | collective-permute-done | bytes 1048608 | tf_op jit(solution)/shard_map/ppermute | solution.py:293
  93.2 12.2 %collective-permute-done.13.refs_6_ = f32[256,512]{1,0:T(8,128)S(1)} collective-permute-done((f32[256,512]{1,0:T(8,128)}, f32[256,512]{1,0:T(8,128)S(1)}, u32[]{:S(2)}, u32[]{:S(2)}) %collective-permute-start.13) | collective-permute-done | bytes 524320 | tf_op jit(solution)/shard_map/ppermute | solution.py:293
  107.4 9.0 %collective-permute-done.10.refs_3_ = f32[256,512]{1,0:T(8,128)S(1)} collective-permute-done((f32[256,512]{1,0:T(8,128)S(1)}, f32[256,512]{1,0:T(8,128)S(1)}, u32[]{:S(2)}, u32[]{:S(2)}) %collective-permute-start.10) | collective-permute-done | bytes 524320 | tf_op jit(solution)/shard_map/ppermute | solution.py:293
  117.2 10.8 %collective-permute-done.14.refs_7_ = f32[256,512]{1,0:T(8,128)S(1)} collective-permute-done((f32[256,512]{1,0:T(8,128)S(1)}, f32[256,512]{1,0:T(8,128)S(1)}, u32[]{:S(2)}, u32[]{:S(2)}) %collective-permute-start.14) | collective-permute-done | bytes 524320 | tf_op jit(solution)/shard_map/ppermute | solution.py:293
  129.0 4.9 shard_map.37
  135.7 18.7 %collective-permute-done.34.refs_6_ = f32[512,512]{1,0:T(8,128)} collective-permute-done((f32[512,512]{1,0:T(8,128)}, f32[512,512]{1,0:T(8,128)}, u32[]{:S(2)}, u32[]{:S(2)}) %collective-permute-start.34) | collective-permute-done | bytes 1048608 | tf_op jit(solution)/shard_map/ppermute | solution.py:293
  154.9 30.0 %shard_map.38 = (f32[512,2048]{1,0:T(8,128)}, f32[512,128]{1,0:T(8,128)}) custom-call(f32[512,512]{1,0:T(8,128)} %copy-done.5, f32[512,512]{1,0:T(8,128)} %copy-done.47, f32[512,512]{1,0:T(8,128)} %collective-permute-done.37.refs_2_, f32[512,512]{1,0:T(8,128)} %collective-permute-done.38.refs_3_, f32[512,512]{1,0:T(8,128)} %collective-permute-done.39.refs_4_, ...), custom_call_target="tpu_custom_call" | custom-call | flops 12884901888 | bytes 20971520 | tf_op jit(solution)/shard_map/pallas_call | solution.py:104
  187.0 12.3 %collective-permute-done.27.refs_6_ = f32[512,512]{1,0:T(8,128)} collective-permute-done((f32[512,512]{1,0:T(8,128)}, f32[512,512]{1,0:T(8,128)}, u32[]{:S(2)}, u32[]{:S(2)}) %collective-permute-start.27) | collective-permute-done | bytes 1048608 | tf_op jit(solution)/shard_map/ppermute | solution.py:293
  199.9 29.9 %shard_map.39 = (f32[512,2048]{1,0:T(8,128)}, f32[512,128]{1,0:T(8,128)}) custom-call(f32[512,512]{1,0:T(8,128)} %copy-done.4, f32[512,512]{1,0:T(8,128)} %copy-done.46, f32[512,512]{1,0:T(8,128)} %collective-permute-done.30.refs_2_, f32[512,512]{1,0:T(8,128)} %copy-done.49, f32[512,512]{1,0:T(8,128)} %copy-done.45, ...), custom_call_target="tpu_custom_call", output_to_operand_aliasing={{0}: (10, {}), {1}: (11, {})} | custom-call | flops 12884901888 | bytes 20971520 | tf_op jit(solution)/shard_map/pallas_call | solution.py:104
  232.4 30.1 %shard_map.40 = (f32[512,2048]{1,0:T(8,128)}, f32[512,128]{1,0:T(8,128)}) custom-call(f32[512,512]{1,0:T(8,128)} %copy-done.3, f32[512,512]{1,0:T(8,128)} %copy-done.48, f32[512,512]{1,0:T(8,128)} %collective-permute-done.23.refs_2_, f32[512,512]{1,0:T(8,128)} %collective-permute-done.24.refs_3_, ...), custom_call_target="tpu_custom_call", output_to_operand_aliasing={{0}: (10, {}), {1}: (11, {})} | custom-call | flops 12884901888 | bytes 20971520 | tf_op jit(solution)/shard_map/pallas_call | solution.py:104
  263.9 17.1 %shard_map.41 = (f32[512,2048]{1,0:T(8,128)}, f32[512,128]{1,0:T(8,128)}) custom-call(f32[512,256]{1,0:T(8,128)} %copy-done.40, f32[512,256]{1,0:T(8,128)} %collective-permute-done.15.refs_1_, f32[512,256]{1,0:T(8,128)} %collective-permute-done.16.refs_2_, f32[512,256]{1,0:T(8,128)} %copy-done.53, ...), custom_call_target="tpu_custom_call", output_to_operand_aliasing={{0}: (10, {}), {1}: (11, {})} | custom-call | flops 6442450944 | bytes 16777216 | tf_op jit(solution)/shard_map/pallas_call | solution.py:104
  282.0 17.3 %shard_map.42 = (f32[512,2048]{1,0:T(8,128)}, f32[512,128]{1,0:T(8,128)}) custom-call(f32[512,256]{1,0:T(8,128)} %get-tuple-element.38.refs_0_, f32[512,256]{1,0:T(8,128)} %copy-done.54, f32[512,256]{1,0:T(8,128)} %collective-permute-done.1.refs_2_, f32[512,256]{1,0:T(8,128)} %copy-done.55, ...), custom_call_target="tpu_custom_call", output_to_operand_aliasing={{0}: (10, {}), {1}: (11, {})} | custom-call | flops 6442450944 | bytes 16777216 | tf_op jit(solution)/shard_map/pallas_call | solution.py:104
  304.9 21.1 %collective-permute-done.43 = f32[256,1024]{1,0:T(8,128)} collective-permute-done((f32[256,1024]{1,0:T(8,128)S(1)}, f32[256,1024]{1,0:T(8,128)}, u32[]{:S(2)}, u32[]{:S(2)}) %collective-permute-start.43) | collective-permute-done | bytes 1048608 | tf_op jit(solution)/shard_map/ppermute | solution.py:293
  335.0 10.7 %collective-permute-done.49 = f32[2,256]{1,0:T(2,128)S(1)} collective-permute-done((f32[2,256]{1,0:T(2,128)S(1)}, f32[2,256]{1,0:T(2,128)S(1)}, u32[]{:S(2)}, u32[]{:S(2)}) %collective-permute-start.49) | collective-permute-done | bytes 2080 | tf_op jit(solution)/shard_map/ppermute | solution.py:293
  346.4 3.0 collective-permute-done.50
  359.3 13.2 %collective-permute-done.45 = f32[64,1024]{1,0:T(8,128)S(1)} collective-permute-done((f32[64,1024]{1,0:T(8,128)S(1)}, f32[64,1024]{1,0:T(8,128)S(1)}, u32[]{:S(2)}, u32[]{:S(2)}) %collective-permute-start.45) | collective-permute-done | bytes 262176 | tf_op jit(solution)/shard_map/ppermute | solution.py:293
  372.5 4.5 collective-permute-done.48
  377.3 3.5 collective-permute-start.53
  381.9 20.5 %collective-permute-done.55.refs_5_ = f32[64,2048]{1,0:T(8,128)S(1)} collective-permute-done((f32[64,2048]{1,0:T(8,128)S(1)}, f32[64,2048]{1,0:T(8,128)S(1)}, u32[]{:S(2)}, u32[]{:S(2)}) %collective-permute-start.55) | collective-permute-done | bytes 524320 | tf_op jit(solution)/shard_map/ppermute | solution.py:293
  406.5 8.5 %collective-permute-done.61.refs_11_ = f32[64,2048]{1,0:T(8,128)S(1)} collective-permute-done((f32[64,2048]{1,0:T(8,128)S(1)}, f32[64,2048]{1,0:T(8,128)S(1)}, u32[]{:S(2)}, u32[]{:S(2)}) %collective-permute-start.61) | collective-permute-done | bytes 524320 | tf_op jit(solution)/shard_map/ppermute | solution.py:293
  418.5 10.0 %collective-permute-done.65.refs_15_ = f32[64,2048]{1,0:T(8,128)S(1)} collective-permute-done((f32[64,2048]{1,0:T(8,128)S(1)}, f32[64,2048]{1,0:T(8,128)S(1)}, u32[]{:S(2)}, u32[]{:S(2)}) %collective-permute-start.65) | collective-permute-done | bytes 524320 | tf_op jit(solution)/shard_map/ppermute | solution.py:293
  429.0 9.1 %collective-permute-done.71.refs_21_ = f32[64,2048]{1,0:T(8,128)S(1)} collective-permute-done((f32[64,2048]{1,0:T(8,128)S(1)}, f32[64,2048]{1,0:T(8,128)S(1)}, u32[]{:S(2)}, u32[]{:S(2)}) %collective-permute-start.71) | collective-permute-done | bytes 524320 | tf_op jit(solution)/shard_map/ppermute | solution.py:293
  442.2 10.7 %collective-permute-done.73.refs_23_ = f32[64,2048]{1,0:T(8,128)S(1)} collective-permute-done((f32[64,2048]{1,0:T(8,128)S(1)}, f32[64,2048]{1,0:T(8,128)S(1)}, u32[]{:S(2)}, u32[]{:S(2)}) %collective-permute-start.73) | collective-permute-done | bytes 524320 | tf_op jit(solution)/shard_map/ppermute | solution.py:293
  454.7 9.0 %collective-permute-done.77.refs_27_ = f32[64,2048]{1,0:T(8,128)S(1)} collective-permute-done((f32[64,2048]{1,0:T(8,128)S(1)}, f32[64,2048]{1,0:T(8,128)S(1)}, u32[]{:S(2)}, u32[]{:S(2)}) %collective-permute-start.77) | collective-permute-done | bytes 524320 | tf_op jit(solution)/shard_map/ppermute | solution.py:293
  467.2 11.4 %collective-permute-done.81.refs_31_ = f32[64,2048]{1,0:T(8,128)S(1)} collective-permute-done((f32[64,2048]{1,0:T(8,128)S(1)}, f32[64,2048]{1,0:T(8,128)S(1)}, u32[]{:S(2)}, u32[]{:S(2)}) %collective-permute-start.81) | collective-permute-done | bytes 524320 | tf_op jit(solution)/shard_map/ppermute | solution.py:293
  480.9 93.0 %shard_map.43 = f32[64,2048]{1,0:T(8,128)} custom-call(s32[39]{0:T(128)} %constant.195.clone.refs_0_, f32[64,2048]{1,0:T(8,128)} %copy-done.2, f32[64,2048]{1,0:T(8,128)} %copy-done.13, f32[64,2048]{1,0:T(8,128)} %copy-done.10, f32[64,2048]{1,0:T(8,128)} %copy-done.20, f32[64,2048]{1,0:T(8,128)} %copy-done.9, f32[64,2048]{1,0:T(8,128)} %copy-done.21, ...), custom_call_target="tpu_custom_call" | custom-call | tf_op jit(solution)/shard_map/pallas_call | solution.py:252
  578.5 2.9 collective-permute-done.83
  (290 shorter events, 97.7 us)
Async XLA Ops:
  9.2 35.5 %collective-permute-start.11 = (f32[256,512]{1,0:T(8,128)S(1)}, f32[256,512]{1,0:T(8,128)}, u32[]{:S(2)}, u32[]{:S(2)}) collective-permute-start(f32[256,512]{1,0:T(8,128)S(1)} %maximum_select_fusion.refs_0_), channel_id=1, source_target_pairs={{0,8},{1,9},{2,10},{3,11},{4,12},{5,13},{6,14},{7,15},{8,0},{9,1},... | collective-permute-start | bytes 1572872 | tf_op jit(solution)/shard_map/ppermute | solution.py:293
  22.2 44.9 %collective-permute-start.37 = (f32[512,512]{1,0:T(8,128)S(1)}, f32[512,512]{1,0:T(8,128)}, u32[]{:S(2)}, u32[]{:S(2)}) collective-permute-start(f32[512,512]{1,0:T(8,128)S(1)} %get-tuple-element.29), channel_id=1, source_target_pairs={{0,8},{1,9},{2,10},{3,11},{4,12},{5,13},{6,14},{7,15},{8,0},{9,1},... | collective-permute-start | bytes 3145736 | tf_op jit(solution)/shard_map/ppermute | solution.py:293
  33.4 33.7 %collective-permute-start.39 = (f32[512,512]{1,0:T(8,128)S(1)}, f32[512,512]{1,0:T(8,128)}, u32[]{:S(2)}, u32[]{:S(2)}) collective-permute-start(f32[512,512]{1,0:T(8,128)S(1)} %get-tuple-element.34.refs_0_), channel_id=1, source_target_pairs={{0,16},{1,17},{2,18},{3,19},{4,20},{5,21},{6,22},{7,23},{8,24},{9,... | collective-permute-start | bytes 3145736 | tf_op jit(solution)/shard_map/ppermute | solution.py:293
  47.2 41.8 %collective-permute-start.30 = (f32[512,512]{1,0:T(8,128)S(1)}, f32[512,512]{1,0:T(8,128)}, u32[]{:S(2)}, u32[]{:S(2)}) collective-permute-start(f32[512,512]{1,0:T(8,128)S(1)} %get-tuple-element.30), channel_id=1, source_target_pairs={{0,8},{1,9},{2,10},{3,11},{4,12},{5,13},{6,14},{7,15},{8,0},{9,1},... | collective-permute-start | bytes 3145736 | tf_op jit(solution)/shard_map/ppermute | solution.py:293
  49.6 42.0 %collective-permute-start.32 = (f32[512,512]{1,0:T(8,128)S(1)}, f32[512,512]{1,0:T(8,128)S(1)}, u32[]{:S(2)}, u32[]{:S(2)}) collective-permute-start(f32[512,512]{1,0:T(8,128)S(1)} %get-tuple-element.31.refs_0_), channel_id=1, source_target_pairs={{0,16},{1,17},{2,18},{3,19},{4,20},{5,21},{6,22},{7,23},{8,24},{9,... | collective-permute-start | bytes 3145736 | tf_op jit(solution)/shard_map/ppermute | solution.py:293
  67.1 38.7 %collective-permute-start.29 = (f32[512,512]{1,0:T(8,128)S(1)}, f32[512,512]{1,0:T(8,128)S(1)}, u32[]{:S(2)}, u32[]{:S(2)}) collective-permute-start(f32[512,512]{1,0:T(8,128)S(1)} %get-tuple-element.31.refs_0_), channel_id=1, source_target_pairs={{0,1},{1,0},{2,3},{3,2},{4,5},{5,4},{6,7},{7,6},{8,9},{9,8},{10,11... | collective-permute-start | bytes 3145736 | tf_op jit(solution)/shard_map/ppermute | solution.py:293
  67.1 38.2 %collective-permute-start.13 = (f32[256,512]{1,0:T(8,128)}, f32[256,512]{1,0:T(8,128)S(1)}, u32[]{:S(2)}, u32[]{:S(2)}) collective-permute-start(f32[256,512]{1,0:T(8,128)} %collective-permute-done.11.refs_4_), channel_id=1, source_target_pairs={{0,4},{1,5},{2,6},{3,7},{4,0},{5,1},{6,2},{7,3},{8,12},{9,13},{10,... | collective-permute-start | bytes 1572872 | tf_op jit(solution)/shard_map/ppermute | solution.py:293
  69.7 59.2 %collective-permute-start.41 = (f32[512,512]{1,0:T(8,128)}, f32[512,512]{1,0:T(8,128)}, u32[]{:S(2)}, u32[]{:S(2)}) collective-permute-start(f32[512,512]{1,0:T(8,128)} %collective-permute-done.37.refs_2_), channel_id=1, source_target_pairs={{0,16},{1,17},{2,18},{3,19},{4,20},{5,21},{6,22},{7,23},{8,24},{9,... | collective-permute-start | bytes 3145736 | tf_op jit(solution)/shard_map/ppermute | solution.py:293
  89.0 27.4 %collective-permute-start.10 = (f32[256,512]{1,0:T(8,128)S(1)}, f32[256,512]{1,0:T(8,128)S(1)}, u32[]{:S(2)}, u32[]{:S(2)}) collective-permute-start(f32[256,512]{1,0:T(8,128)S(1)} %collective-permute-done.8.refs_1_), channel_id=1, source_target_pairs={{0,4},{1,5},{2,6},{3,7},{4,0},{5,1},{6,2},{7,3},{8,12},{9,13},{10,... | collective-permute-start | bytes 1572872 | tf_op jit(solution)/shard_map/ppermute | solution.py:293
  91.6 25.6 %collective-permute-start.12 = (f32[256,512]{1,0:T(8,128)}, f32[256,512]{1,0:T(8,128)S(1)}, u32[]{:S(2)}, u32[]{:S(2)}) collective-permute-start(f32[256,512]{1,0:T(8,128)} %collective-permute-done.11.refs_4_), channel_id=1, source_target_pairs={{0,2},{1,3},{2,0},{3,1},{4,6},{5,7},{6,4},{7,5},{8,10},{9,11},{10,... | collective-permute-start | bytes 1572872 | tf_op jit(solution)/shard_map/ppermute | solution.py:293
  105.9 28.1 %collective-permute-start.23 = (f32[512,512]{1,0:T(8,128)}, f32[512,512]{1,0:T(8,128)}, u32[]{:S(2)}, u32[]{:S(2)}) collective-permute-start(f32[512,512]{1,0:T(8,128)} %get-tuple-element.32), channel_id=1, source_target_pairs={{0,8},{1,9},{2,10},{3,11},{4,12},{5,13},{6,14},{7,15},{8,0},{9,1},... | collective-permute-start | bytes 3145736 | tf_op jit(solution)/shard_map/ppermute | solution.py:293
  128.0 26.3 %collective-permute-start.34 = (f32[512,512]{1,0:T(8,128)}, f32[512,512]{1,0:T(8,128)}, u32[]{:S(2)}, u32[]{:S(2)}) collective-permute-start(f32[512,512]{1,0:T(8,128)} %collective-permute-done.30.refs_2_), channel_id=1, source_target_pairs={{0,16},{1,17},{2,18},{3,19},{4,20},{5,21},{6,22},{7,23},{8,24},{9,... | collective-permute-start | bytes 3145736 | tf_op jit(solution)/shard_map/ppermute | solution.py:293
  128.9 25.9 %collective-permute-start.42 = (f32[512,512]{1,0:T(8,128)}, f32[512,512]{1,0:T(8,128)}, u32[]{:S(2)}, u32[]{:S(2)}) collective-permute-start(f32[512,512]{1,0:T(8,128)} %collective-permute-done.41.refs_6_), channel_id=1, source_target_pairs={{0,1},{1,0},{2,3},{3,2},{4,5},{5,4},{6,7},{7,6},{8,9},{9,8},{10,11... | collective-permute-start | bytes 3145736 | tf_op jit(solution)/shard_map/ppermute | solution.py:293
  134.0 50.9 %collective-permute-start.25 = (f32[512,512]{1,0:T(8,128)S(1)}, f32[512,512]{1,0:T(8,128)}, u32[]{:S(2)}, u32[]{:S(2)}) collective-permute-start(f32[512,512]{1,0:T(8,128)S(1)} %get-tuple-element.33.refs_0_), channel_id=1, source_target_pairs={{0,16},{1,17},{2,18},{3,19},{4,20},{5,21},{6,22},{7,23},{8,24},{9,... | collective-permute-start | bytes 3145736 | tf_op jit(solution)/shard_map/ppermute | solution.py:293
  135.2 50.3 %collective-permute-start.31 = (f32[512,512]{1,0:T(8,128)}, f32[512,512]{1,0:T(8,128)S(1)}, u32[]{:S(2)}, u32[]{:S(2)}) collective-permute-start(f32[512,512]{1,0:T(8,128)} %collective-permute-done.30.refs_2_), channel_id=1, source_target_pairs={{0,1},{1,0},{2,3},{3,2},{4,5},{5,4},{6,7},{7,6},{8,9},{9,8},{10,11... | collective-permute-start | bytes 3145736 | tf_op jit(solution)/shard_map/ppermute | solution.py:293
  135.4 51.7 %collective-permute-start.33 = (f32[512,512]{1,0:T(8,128)}, f32[512,512]{1,0:T(8,128)}, u32[]{:S(2)}, u32[]{:S(2)}) collective-permute-start(f32[512,512]{1,0:T(8,128)} %copy-done.45), channel_id=1, source_target_pairs={{0,1},{1,0},{2,3},{3,2},{4,5},{5,4},{6,7},{7,6},{8,9},{9,8},{10,11... | collective-permute-start | bytes 3145736 | tf_op jit(solution)/shard_map/ppermute | solution.py:293
  154.4 44.9 %collective-permute-start.27 = (f32[512,512]{1,0:T(8,128)}, f32[512,512]{1,0:T(8,128)}, u32[]{:S(2)}, u32[]{:S(2)}) collective-permute-start(f32[512,512]{1,0:T(8,128)} %collective-permute-done.23.refs_2_), channel_id=1, source_target_pairs={{0,16},{1,17},{2,18},{3,19},{4,20},{5,21},{6,22},{7,23},{8,24},{9,... | collective-permute-start | bytes 3145736 | tf_op jit(solution)/shard_map/ppermute | solution.py:293
  154.8 44.5 %collective-permute-start.35 = (f32[512,512]{1,0:T(8,128)}, f32[512,512]{1,0:T(8,128)}, u32[]{:S(2)}, u32[]{:S(2)}) collective-permute-start(f32[512,512]{1,0:T(8,128)} %collective-permute-done.34.refs_6_), channel_id=1, source_target_pairs={{0,1},{1,0},{2,3},{3,2},{4,5},{5,4},{6,7},{7,6},{8,9},{9,8},{10,11... | collective-permute-start | bytes 3145736 | tf_op jit(solution)/shard_map/ppermute | solution.py:293
  184.9 44.9 %collective-permute-start.22 = (f32[512,512]{1,0:T(8,128)S(1)}, f32[512,512]{1,0:T(8,128)S(1)}, u32[]{:S(2)}, u32[]{:S(2)}) collective-permute-start(f32[512,512]{1,0:T(8,128)S(1)} %get-tuple-element.33.refs_0_), channel_id=1, source_target_pairs={{0,1},{1,0},{2,3},{3,2},{4,5},{5,4},{6,7},{7,6},{8,9},{9,8},{10,11... | collective-permute-start | bytes 3145736 | tf_op jit(solution)/shard_map/ppermute | solution.py:293
  185.4 44.9 %collective-permute-start.20 = (f32[512,256]{1,0:T(8,128)}, f32[512,256]{1,0:T(8,128)S(1)}, u32[]{:S(2)}, u32[]{:S(2)}) collective-permute-start(f32[512,256]{1,0:T(8,128)} %collective-permute-done.16.refs_2_), channel_id=1, source_target_pairs={{0,16},{1,17},{2,18},{3,19},{4,20},{5,21},{6,22},{7,23},{8,24},{9,... | collective-permute-start | bytes 1572872 | tf_op jit(solution)/shard_map/ppermute | solution.py:293
  187.0 43.3 %collective-permute-start.24 = (f32[512,512]{1,0:T(8,128)}, f32[512,512]{1,0:T(8,128)}, u32[]{:S(2)}, u32[]{:S(2)}) collective-permute-start(f32[512,512]{1,0:T(8,128)} %collective-permute-done.23.refs_2_), channel_id=1, source_target_pairs={{0,1},{1,0},{2,3},{3,2},{4,5},{5,4},{6,7},{7,6},{8,9},{9,8},{10,11... | collective-permute-start | bytes 3145736 | tf_op jit(solution)/shard_map/ppermute | solution.py:293
  199.3 31.5 %collective-permute-start.26 = (f32[512,512]{1,0:T(8,128)}, f32[512,512]{1,0:T(8,128)}, u32[]{:S(2)}, u32[]{:S(2)}) collective-permute-start(f32[512,512]{1,0:T(8,128)} %collective-permute-done.25.refs_4_), channel_id=1, source_target_pairs={{0,1},{1,0},{2,3},{3,2},{4,5},{5,4},{6,7},{7,6},{8,9},{9,8},{10,11... | collective-permute-start | bytes 3145736 | tf_op jit(solution)/shard_map/ppermute | solution.py:293
  199.3 33.1 %collective-permute-start.28 = (f32[512,512]{1,0:T(8,128)}, f32[512,512]{1,0:T(8,128)}, u32[]{:S(2)}, u32[]{:S(2)}) collective-permute-start(f32[512,512]{1,0:T(8,128)} %collective-permute-done.27.refs_6_), channel_id=1, source_target_pairs={{0,1},{1,0},{2,3},{3,2},{4,5},{5,4},{6,7},{7,6},{8,9},{9,8},{10,11... | collective-permute-start | bytes 3145736 | tf_op jit(solution)/shard_map/ppermute | solution.py:293
  229.8 32.7 %collective-permute-start.3 = (f32[512,256]{1,0:T(8,128)S(1)}, f32[512,256]{1,0:T(8,128)S(1)}, u32[]{:S(2)}, u32[]{:S(2)}) collective-permute-start(f32[512,256]{1,0:T(8,128)S(1)} %copy-done.39), channel_id=1, source_target_pairs={{0,16},{1,17},{2,18},{3,19},{4,20},{5,21},{6,22},{7,23},{8,24},{9,... | collective-permute-start | bytes 1572872 | tf_op jit(solution)/shard_map/ppermute | solution.py:293
  230.3 32.8 %collective-permute-start.17 = (f32[512,256]{1,0:T(8,128)}, f32[512,256]{1,0:T(8,128)S(1)}, u32[]{:S(2)}, u32[]{:S(2)}) collective-permute-start(f32[512,256]{1,0:T(8,128)} %collective-permute-done.16.refs_2_), channel_id=1, source_target_pairs={{0,1},{1,0},{2,3},{3,2},{4,5},{5,4},{6,7},{7,6},{8,9},{9,8},{10,11... | collective-permute-start | bytes 1572872 | tf_op jit(solution)/shard_map/ppermute | solution.py:293
  230.4 32.9 %collective-permute-start.19 = (f32[512,256]{1,0:T(8,128)}, f32[512,256]{1,0:T(8,128)}, u32[]{:S(2)}, u32[]{:S(2)}) collective-permute-start(f32[512,256]{1,0:T(8,128)} %collective-permute-done.18.refs_4_), channel_id=1, source_target_pairs={{0,1},{1,0},{2,3},{3,2},{4,5},{5,4},{6,7},{7,6},{8,9},{9,8},{10,11... | collective-permute-start | bytes 1572872 | tf_op jit(solution)/shard_map/ppermute | solution.py:293
  230.9 32.8 %collective-permute-start.5 = (f32[512,256]{1,0:T(8,128)}, f32[512,256]{1,0:T(8,128)S(1)}, u32[]{:S(2)}, u32[]{:S(2)}) collective-permute-start(f32[512,256]{1,0:T(8,128)} %collective-permute-done.1.refs_2_), channel_id=1, source_target_pairs={{0,16},{1,17},{2,18},{3,19},{4,20},{5,21},{6,22},{7,23},{8,24},{9,... | collective-permute-start | bytes 1572872 | tf_op jit(solution)/shard_map/ppermute | solution.py:293
  232.4 31.3 %collective-permute-start.21 = (f32[512,256]{1,0:T(8,128)S(1)}, f32[512,256]{1,0:T(8,128)}, u32[]{:S(2)}, u32[]{:S(2)}) collective-permute-start(f32[512,256]{1,0:T(8,128)S(1)} %collective-permute-done.20.refs_6_), channel_id=1, source_target_pairs={{0,1},{1,0},{2,3},{3,2},{4,5},{5,4},{6,7},{7,6},{8,9},{9,8},{10,11... | collective-permute-start | bytes 1572872 | tf_op jit(solution)/shard_map/ppermute | solution.py:293
  300.6 25.5 %collective-permute-start.43 = (f32[256,1024]{1,0:T(8,128)S(1)}, f32[256,1024]{1,0:T(8,128)}, u32[]{:S(2)}, u32[]{:S(2)}) collective-permute-start(f32[256,1024]{1,0:T(8,128)S(1)} %slice_bitcast_fusion), channel_id=1, source_target_pairs={{0,8},{1,9},{2,10},{3,11},{4,12},{5,13},{6,14},{7,15},{8,0},{9,1},... | collective-permute-start | bytes 3145736 | tf_op jit(solution)/shard_map/ppermute | solution.py:293
  304.9 25.3 %collective-permute-start.46 = (f32[2,128,1024]{2,1,0:T(8,128)}, f32[2,128,1024]{2,1,0:T(8,128)}, u32[]{:S(2)}, u32[]{:S(2)}) collective-permute-start(f32[2,128,1024]{2,1,0:T(8,128)} %constant_dynamic-slice_fusion.3), channel_id=1, source_target_pairs={{0,2},{1,3},{2,0},{3,1},{4,6},{5,7},{6,4},{7,5},{8,10},{9,11},{10,... | collective-permute-start | bytes 3145736 | tf_op jit(solution)/shard_map/ppermute | solution.py:293
  328.6 25.3 %collective-permute-start.44 = (f32[128,1024]{1,0:T(8,128)}, f32[128,1024]{1,0:T(8,128)}, u32[]{:S(2)}, u32[]{:S(2)}) collective-permute-start(f32[128,1024]{1,0:T(8,128)} %constant_dynamic-slice_fusion.5), channel_id=1, source_target_pairs={{0,2},{1,3},{2,0},{3,1},{4,6},{5,7},{6,4},{7,5},{8,10},{9,11},{10,... | collective-permute-start | bytes 1572872 | tf_op jit(solution)/shard_map/ppermute | solution.py:293
  377.2 25.2 %collective-permute-start.55 = (f32[64,2048]{1,0:T(8,128)S(1)}, f32[64,2048]{1,0:T(8,128)S(1)}, u32[]{:S(2)}, u32[]{:S(2)}) collective-permute-start(f32[64,2048]{1,0:T(8,128)S(1)} %fusion.2.refs_1_), channel_id=1, source_target_pairs={{0,4},{1,5},{2,6},{3,7},{4,0},{5,1},{6,2},{7,3},{8,12},{9,13},{10,... | collective-permute-start | bytes 1572872 | tf_op jit(solution)/shard_map/ppermute | solution.py:293
  (110 other events, 2843.1 us)
